TPU v7x, 128 devices: a whole 4x4x4 slice. The times are simulated.
128 devices in a mesh: ty: 16 (over x, y), tx: 8 (over z, core).
Axes of the slice: x: 4, y: 4, z: 4, core: 2. Of those that a mesh axis runs over, the one named last changes fastest.
Arguments:
- potential: float32 [4, 4096, 2048], P(None, 'ty', 'tx'), may hold values from -6 to 6
- probe: float32 [2, 256, 256], replicated, may hold values from -4.2 to 4.2
- patterns: bfloat16 [256, 256, 256], P(('ty', 'tx')), may hold values from 0 to 12
- scan_centers: int32 [256, 2], P(('ty', 'tx')), may hold values from 128 to 3967, as said below
Outputs:
- potential_grad: float32 [4, 4096, 2048], P(None, 'ty', 'tx')
Inputs may be any that keep to these rules, and one draw needn't show every extreme that they name: `scan_centers`: rows of the device at index i of ty (blocks of 2 rows per device, ty slowest) have their first entry in [i * 256, (i + 1) * 256); the second entries of one device's rows lie in distinct column tiles of 256 cells; in each index of ty some column tile is named by every device of that index; every window of 256 x 256 cells around a centre lies inside the object.
All inputs are finite; a program needn't handle non-finite values.
Results may differ from a plain program's by a relative error of at most 0.035.
The roundings to bfloat16 on the way count: a program that leaves them out, or rounds other values in their place, can miss the bound.
Values may be sent and summed in bfloat16 or wider, within the bound.
No kernel may reach another device: no remote copies, remote signals or barrier semaphores. Data moves between devices by JAX's collectives and lax.ppermute only.
A program may use at most 128 MiB of HBM per device.

v0:
```python
import functools
import math

import jax
import jax.numpy as jnp
import numpy as np
from jax import lax
from jax.experimental import pallas as pl
from jax.experimental.pallas import tpu as pltpu
from jax.sharding import PartitionSpec as P

fresnel = 41.0
band_reach = 20.0
SLOT_PAD = 16
TILE = 256
LANES = 128
PITCH = 5


def sin_cos_coefs(limit):
    nodes = np.cos((np.arange(512) + 0.5) * np.pi / 512)
    u = 0.5 * (nodes + 1.0)
    v = np.sqrt(u) * limit
    t = 0.5 * v
    sinc = np.where(t == 0, 0.5, np.sin(t) / np.where(v == 0, 1.0, v))
    scale = limit * limit
    a = np.polynomial.polynomial.polyfit(u, sinc, 6) / scale ** np.arange(7)
    b = np.polynomial.polynomial.polyfit(u, np.cos(t), 7) / scale ** np.arange(8)
    return [float(np.float32(x)) for x in a], [float(np.float32(x)) for x in b]


SIN_COEFS, COS_COEFS = sin_cos_coefs(6.0)


def sin_cos_half(v):
    u = v * v
    s = SIN_COEFS[-1]
    for a in SIN_COEFS[-2::-1]:
        s = s * u + a
    c = COS_COEFS[-1]
    for b in COS_COEFS[-2::-1]:
        c = c * u + b
    return s * v, c


def make_tables(length):
    f32 = np.float32
    indices = np.arange(length, dtype=np.int32)
    gap = (indices[:, None] - indices[None, :]).astype(f32)
    chirp = f32(math.pi) * gap * gap / f32(fresnel)
    amplitude = (np.abs(gap) <= band_reach).astype(f32) / f32(math.sqrt(fresnel))
    product = indices[:, None] * indices[None, :] % length
    angle = f32(-2.0 * math.pi) * product.astype(f32) / f32(length)
    norm = f32(1.0 / math.sqrt(length))
    pairs = [
        (amplitude * np.cos(chirp), amplitude * np.sin(chirp)),
        (np.cos(angle) * norm, np.sin(angle) * norm),
    ]
    tables = []
    for re, im in pairs:
        left = np.block([[re, -im], [im, re]])
        right = np.block([[re, im], [-im, re]])
        tables += [left.astype(jnp.bfloat16), right.astype(jnp.bfloat16)]
    return np.stack(tables)


def windows_kernel(
    half, where_ref, own_hbm, up_ref, down_ref, west_ref, east_ref, probe_hbm, pat_hbm, tab_hbm,
    mid_ref, wout_ref, eout_ref,
    ext_ref, acc_ref, order_ref, own_ref, probe_ref, pat_ref, tab_ref, sems, *streams,
):
    loads = [
        pltpu.make_async_copy(own_hbm, own_ref, sems.at[0]),
        pltpu.make_async_copy(tab_hbm, tab_ref, sems.at[1]),
        pltpu.make_async_copy(probe_hbm, probe_ref, sems.at[2]),
        pltpu.make_async_copy(pat_hbm, pat_ref, sems.at[3]),
    ]
    for load in loads:
        load.start()
    slices, tile_y, tile_x = own_ref.shape
    width = probe_ref.shape[1]
    slots = pat_ref.shape[0]
    rows = 64
    f32, bf16 = jnp.float32, jnp.bfloat16
    tall = tile_y + width
    blocks = (tile_x + width) // LANES
    side = half // LANES
    halves = width // LANES

    def every(start, count, block):
        return pl.ds(start * PITCH + block, count, stride=PITCH)

    for s in range(slices):
        for c in range(side):
            lanes = slice(c * LANES, (c + 1) * LANES)
            ext_ref[s, every(0, tall, c)] = west_ref[s, :, lanes].astype(f32)
            ext_ref[s, every(0, tall, blocks - side + c)] = east_ref[s, :, lanes].astype(f32)
        for c in range(blocks - 2 * side):
            lanes = slice(c * LANES, (c + 1) * LANES)
            ext_ref[s, every(0, half, side + c)] = up_ref[s, :, lanes].astype(f32)
            ext_ref[s, every(half + tile_y, half, side + c)] = down_ref[s, :, lanes].astype(f32)
        acc_ref[s] = jnp.zeros(acc_ref.shape[1:], f32)
    loads[0].wait()
    for s in range(slices):
        for c in range(blocks - 2 * side):
            inner = own_ref[s, :, c * LANES : (c + 1) * LANES].astype(bf16).astype(f32)
            ext_ref[s, every(half, tile_y, side + c)] = inner
    for load in loads[1:]:
        load.wait()

    def dot(a, b):
        return jnp.dot(a, b, preferred_element_type=f32)

    def chunks():
        return [slice(k * rows, (k + 1) * rows) for k in range(width // rows)]

    def one_window(slot, cs_ref, phi_ref, s_ref, t_ref):
        row = where_ref[slot, 0]
        col = where_ref[slot, 1]
        block = col // LANES
        turn = col - block * LANES
        back = jnp.where(turn == 0, 0, LANES - turn)
        lane = lax.broadcasted_iota(jnp.int32, (rows, LANES), 1)
        low = lane < LANES - turn
        high = lane >= turn

        def modulate(s, k, re, im):
            parts = [
                pltpu.roll(ext_ref[s, every(row + k.start, rows, block + j)], back, 1)
                for j in range(halves + 1)
            ]
            for j in range(halves):
                c = slice(j * LANES, (j + 1) * LANES)
                sin, cos = sin_cos_half(jnp.where(low, parts[j], parts[j + 1]))
                cs_ref[s, 0, k, c] = cos
                cs_ref[s, 1, k, c] = sin
                new_re = re[:, c] * cos - im[:, c] * sin
                new_im = re[:, c] * sin + im[:, c] * cos
                phi_ref[s, 0, k, c] = new_re
                phi_ref[s, 1, k, c] = new_im
                s_ref[k, c] = new_re.astype(bf16)
                s_ref[width + k.start : width + k.stop, c] = new_im.astype(bf16)

        def deposit(s, k, grad):
            parts = [pltpu.roll(grad[:, j * LANES : (j + 1) * LANES], turn, 1) for j in range(halves)]
            zero = jnp.zeros((rows, LANES), f32)
            for j in range(halves + 1):
                here = parts[j] if j < halves else zero
                before = parts[j - 1] if j else zero
                acc_ref[s, every(row + k.start, rows, block + j)] += jnp.where(high, here, before)

        def apply(table):
            mid = dot(tab_ref[table], s_ref[...]).astype(bf16)
            t_ref[:, :width] = mid[:width]
            t_ref[:, width:] = mid[width:]
            return dot(t_ref[...], tab_ref[table + 1])

        def apply_back(table):
            mid = dot(t_ref[...], tab_ref[table]).astype(bf16)
            s_ref[:width] = mid[:, :width]
            s_ref[width:] = mid[:, width:]
            return dot(tab_ref[table + 1], s_ref[...])

        for k in chunks():
            modulate(0, k, probe_ref[0, k], probe_ref[1, k])
        for s in range(1, slices):
            yield
            z = apply(0)
            yield
            for k in chunks():
                modulate(s, k, z[k, :width], z[k, width:])
        yield
        z = apply(2)
        yield
        for k in chunks():
            re, im = z[k, :width], z[k, width:]
            excess = re * re + im * im - pat_ref[slot, k].astype(f32)
            twice = excess + excess
            t_ref[k, :width] = (twice * re).astype(bf16)
            t_ref[k, width:] = (twice * im).astype(bf16)
        for s in range(slices - 1, -1, -1):
            yield
            g = apply_back(2 if s == slices - 1 else 0)
            yield
            for k in chunks():
                re, im = g[k], g[width + k.start : width + k.stop]
                grad = 0.5 * (im * phi_ref[s, 0, k] - re * phi_ref[s, 1, k])
                deposit(s, k, grad)
                if s:
                    cos, sin = cs_ref[s, 0, k], cs_ref[s, 1, k]
                    t_ref[k, :width] = (re * cos + im * sin).astype(bf16)
                    t_ref[k, width:] = (im * cos - re * sin).astype(bf16)

    def list_slot(slot, filled):
        order_ref[filled] = slot
        return filled + where_ref[slot, 2]

    filled = lax.fori_loop(0, slots, list_slot, 0)

    def pair(number, carry):
        first = one_window(order_ref[2 * number], *streams[:4])
        second = one_window(order_ref[2 * number + 1], *streams[4:])
        next(first)
        alive = True
        while alive:
            alive = False
            for stream in (first, second):
                alive = next(stream, True) is None or alive
        return carry

    lax.fori_loop(0, filled // 2, pair, 0)

    @pl.when(filled % 2 == 1)
    def _():
        for _ in one_window(order_ref[filled - 1], *streams[:4]):
            pass

    for s in range(slices):
        for b in range(blocks):
            part = acc_ref[s, every(0, tall, b)]
            if b < side:
                wout_ref[s, :, b * LANES : (b + 1) * LANES] = part.astype(bf16)
            elif b >= blocks - side:
                c = b - (blocks - side)
                eout_ref[s, :, c * LANES : (c + 1) * LANES] = part.astype(bf16)
            else:
                c = b - side
                mid_ref[s, :, c * LANES : (c + 1) * LANES] = part


def run_windows(where, own, up, down, west, east, probe, patterns, tables, interpret=False):
    slices, tile_y, tile_x = own.shape
    width = probe.shape[1]
    half = width // 2
    tall = tile_y + width
    f32, bf16 = jnp.float32, jnp.bfloat16
    vmem = pl.BlockSpec(memory_space=pltpu.VMEM)
    hbm = pl.BlockSpec(memory_space=pltpu.HBM)
    return pl.pallas_call(
        functools.partial(windows_kernel, half),
        out_shape=(
            jax.ShapeDtypeStruct((slices, tall, tile_x), f32),
            jax.ShapeDtypeStruct((slices, tall, half), bf16),
            jax.ShapeDtypeStruct((slices, tall, half), bf16),
        ),
        in_specs=[pl.BlockSpec(memory_space=pltpu.SMEM), hbm] + [vmem] * 4 + [hbm] * 3,
        out_specs=(vmem,) * 3,
        scratch_shapes=[
            pltpu.VMEM((slices, tall * PITCH, LANES), f32),
            pltpu.VMEM((slices, tall * PITCH, LANES), f32),
            pltpu.SMEM((patterns.shape[0] + 1,), jnp.int32),
            pltpu.VMEM(own.shape, f32),
            pltpu.VMEM(probe.shape, f32),
            pltpu.VMEM(patterns.shape, bf16),
            pltpu.VMEM(tables.shape, bf16),
            pltpu.SemaphoreType.DMA((4,)),
        ]
        + [
            pltpu.VMEM((slices, 2, width, width), f32),
            pltpu.VMEM((slices, 2, width, width), f32),
            pltpu.VMEM((2 * width, width), bf16),
            pltpu.VMEM((width, 2 * width), bf16),
        ]
        * 2,
        compiler_params=pltpu.CompilerParams(vmem_limit_bytes=56 << 20),
        interpret=interpret,
    )(where, own, up, down, west, east, probe, patterns, tables)


def edges_kernel(own_ref, up_ref, down_ref, west_ref, east_ref):
    half = up_ref.shape[1]
    tile_y, tile_x = own_ref.shape[1:]
    bf16 = jnp.bfloat16
    up_ref[...] = own_ref[:, :half].astype(bf16)
    down_ref[...] = own_ref[:, tile_y - half :].astype(bf16)
    west_ref[...] = own_ref[:, :, :half].astype(bf16)
    east_ref[...] = own_ref[:, :, tile_x - half :].astype(bf16)


def edges(own, half):
    slices, tile_y, tile_x = own.shape
    bf16 = jnp.bfloat16
    flat = jax.ShapeDtypeStruct((slices, half, tile_x), bf16)
    tall = jax.ShapeDtypeStruct((slices, tile_y, half), bf16)

    def slab(shape):
        return pl.BlockSpec((1,) + shape[1:], lambda s: (s, 0, 0))

    return pl.pallas_call(
        edges_kernel,
        grid=(slices,),
        out_shape=(flat, flat, tall, tall),
        in_specs=[slab(own.shape)],
        out_specs=tuple(slab(x.shape) for x in (flat, flat, tall, tall)),
        compiler_params=pltpu.CompilerParams(vmem_limit_bytes=56 << 20),
    )(own)


def parcel_kernel(centers_ref, pat_ref, sent_ref):
    slots, _, width = sent_ref.shape
    bf16 = jnp.bfloat16
    lane = lax.broadcasted_iota(jnp.int32, (SLOT_PAD, width), 1)
    sent_ref[...] = jnp.zeros(sent_ref.shape, bf16)
    for p in range(pat_ref.shape[0]):
        owner = centers_ref[p, 1] // TILE
        row = centers_ref[p, 0] % TILE
        col = centers_ref[p, 1] % TILE
        info = jnp.where(lane == 0, row, jnp.where(lane == 1, col, jnp.where(lane == 2, 1, 0)))
        sent_ref[owner, :width] = pat_ref[p]
        sent_ref[owner, width:] = info.astype(jnp.float32).astype(bf16)


def parcels(centers, patterns, slots):
    width = patterns.shape[1]
    vmem = pl.BlockSpec(memory_space=pltpu.VMEM)
    return pl.pallas_call(
        parcel_kernel,
        out_shape=jax.ShapeDtypeStruct((slots, width + SLOT_PAD, width), jnp.bfloat16),
        in_specs=[pl.BlockSpec(memory_space=pltpu.SMEM), vmem],
        out_specs=vmem,
        compiler_params=pltpu.CompilerParams(vmem_limit_bytes=56 << 20),
    )(centers, patterns)


def shift(cells, axis, step):
    count = lax.axis_size(axis)
    pairs = [(i, i + step) for i in range(count) if 0 <= i + step < count]
    return lax.ppermute(cells, axis, pairs)


def per_device(tables, potential, probe, patterns, scan_centers):
    slices, tile_y, tile_x = potential.shape
    width = probe.shape[1]
    half = width // 2
    columns = lax.axis_size("tx")
    f32, bf16 = jnp.float32, jnp.bfloat16

    first_rows, last_rows, first_cols, last_cols = edges(potential, half)
    up = shift(last_rows, "ty", 1)
    down = shift(first_rows, "ty", -1)

    sent = parcels(scan_centers, patterns, columns)
    got = lax.all_to_all(sent, "tx", split_axis=0, concat_axis=0, tiled=True)
    where = got[:, width, :3].astype(f32).astype(jnp.int32)

    west = shift(
        jnp.concatenate([up[:, :, tile_x - half :], last_cols, down[:, :, tile_x - half :]], 1), "tx", 1
    )
    east = shift(jnp.concatenate([up[:, :, :half], first_cols, down[:, :, :half]], 1), "tx", -1)

    mid, to_west, to_east = run_windows(
        where, potential, up, down, west, east, probe, got, tables
    )

    from_west = shift(to_east, "tx", 1)
    from_east = shift(to_west, "tx", -1)

    def with_sides(lo, hi):
        add = jnp.concatenate([from_west[:, lo:hi], from_east[:, lo:hi]], 2)
        return mid[:, lo:hi] + add.astype(f32)

    from_up = shift(with_sides(half + tile_y, 2 * half + tile_y).astype(bf16), "ty", 1)
    from_down = shift(with_sides(0, half).astype(bf16), "ty", -1)
    return with_sides(half, half + tile_y) + jnp.concatenate([from_up, from_down], 1).astype(f32)


def solution(mesh):
    in_specs = (P(None, "ty", "tx"), P(), P(("ty", "tx"), None, None), P(("ty", "tx"), None))
    out_specs = P(None, "ty", "tx")

    def run(potential, probe, patterns, scan_centers):
        tables = jnp.asarray(make_tables(probe.shape[1]))
        return jax.shard_map(
            functools.partial(per_device, tables),
            mesh=mesh, in_specs=in_specs, out_specs=out_specs, check_vma=False,
        )(potential, probe, patterns, scan_centers)

    return run
```

profile of v0, /device:TPU:57, one launch (start us, length us, event | category | flops | bytes accessed | tf_op | source)
XLA Modules:
  0.0 101.4 jit_solution(3274725902068264836)
XLA Ops:
  0.0 3.3 %shard_map.56 = (bf16[4,128,256]{2,1,0:T(8,128)(2,1)}, bf16[4,128,256]{2,1,0:T(8,128)(2,1)}, bf16[4,256,128]{2,1,0:T(8,128)(2,1)}, bf16[4,256,128]{2,1,0:T(8,128)(2,1)}) custom-call(f32[4,256,256]{2,1,0:T(8,128)} %own_hbm.1), custom_call_target="tpu_custom_call" | custom-call | tf_op jit(solution)/shard_map/pallas_call | solution.py:289
  3.3 2.8 %collective-permute-start = (bf16[4,128,256]{2,1,0:T(8,128)(2,1)}, bf16[4,128,256]{2,1,0:T(8,128)(2,1)S(1)}, u32[]{:S(2)}, u32[]{:S(2)}) collective-permute-start(bf16[4,128,256]{2,1,0:T(8,128)(2,1)} %get-tuple-element.12), channel_id=1, source_target_pairs={{0,8},{8,16},{16,24},{24,32},{32,40},{40,48},{48,56},{56,64},{64,7... | collective-permute-start | bytes 786440 | tf_op jit(solution)/shard_map/ppermute | solution.py:328
  6.1 0.0 copy-start.6
  6.1 2.6 %collective-permute-start.1 = (bf16[4,128,256]{2,1,0:T(8,128)(2,1)}, bf16[4,128,256]{2,1,0:T(8,128)(2,1)S(1)}, u32[]{:S(2)}, u32[]{:S(2)}) collective-permute-start(bf16[4,128,256]{2,1,0:T(8,128)(2,1)} %get-tuple-element.13), channel_id=1, source_target_pairs={{8,0},{16,8},{24,16},{32,24},{40,32},{48,40},{56,48},{64,56},{72,6... | collective-permute-start | bytes 786440 | tf_op jit(solution)/shard_map/ppermute | solution.py:328
  8.7 2.1 %shard_map.55 = bf16[8,272,256]{2,1,0:T(8,128)(2,1)} custom-call(s32[2,2]{1,0:T(2,128)} %centers_ref.1, bf16[2,256,256]{2,1,0:T(8,128)(2,1)} %pat_ref.1), custom_call_target="tpu_custom_call" | custom-call | tf_op jit(solution)/shard_map/pallas_call | solution.py:316
  10.8 0.0 copy-start.5
  10.8 6.4 %all-to-all-start = ((bf16[8,272,256]{2,1,0:T(8,128)(2,1)}), bf16[8,272,256]{2,1,0:T(8,128)(2,1)S(1)}, u32[]{:S(2)}, u32[]{:S(2)}) async-start(bf16[8,272,256]{2,1,0:T(8,128)(2,1)} %shard_map.55), calls=%async_computation | async-start | bytes 2228224 | tf_op jit(solution)/shard_map/all_to_all | solution.py:343
  17.3 0.0 collective-permute-done.up_ref
  17.3 0.0 copy-start.2
  17.3 0.0 collective-permute-done.1.down_ref
  17.3 0.0 copy-start.3
  17.4 0.0 copy-done.6
  17.5 5.3 %collective-permute-start.2 = (bf16[4,512,128]{2,1,0:T(8,128)(2,1)S(1)}, bf16[4,512,128]{2,1,0:T(8,128)(2,1)S(1)}, u32[]{:S(2)}, u32[]{:S(2)}) collective-permute-start(bf16[4,512,128]{2,1,0:T(8,128)(2,1)S(1)} %pad_maximum_fusion), channel_id=1, source_target_pairs={{0,1},{1,2},{2,3},{3,4},{4,5},{5,6},{6,7},{8,9},{9,10},{10,11},{11... | collective-permute-start | bytes 1572872 | tf_op jit(solution)/shard_map/ppermute | solution.py:328
  22.7 0.0 copy-done.5
  22.8 1.9 %collective-permute-start.3 = (bf16[4,512,128]{2,1,0:T(8,128)(2,1)S(1)}, bf16[4,512,128]{2,1,0:T(8,128)(2,1)}, u32[]{:S(2)}, u32[]{:S(2)}) collective-permute-start(bf16[4,512,128]{2,1,0:T(8,128)(2,1)S(1)} %pad_maximum_fusion.1), channel_id=1, source_target_pairs={{1,0},{2,1},{3,2},{4,3},{5,4},{6,5},{7,6},{9,8},{10,9},{11,10},{12... | collective-permute-start | bytes 1572872 | tf_op jit(solution)/shard_map/ppermute | solution.py:328
  24.7 7.3 %all-to-all-done.pat_hbm = bf16[8,272,256]{2,1,0:T(8,128)(2,1)S(1)} async-done(((bf16[8,272,256]{2,1,0:T(8,128)(2,1)}), bf16[8,272,256]{2,1,0:T(8,128)(2,1)S(1)}, u32[]{:S(2)}, u32[]{:S(2)}) %all-to-all-start) | async-done | bytes 1114144 | tf_op jit(solution)/shard_map/all_to_all | solution.py:343
  32.0 0.0 copy-start
  32.0 0.6 fusion
  32.6 2.7 %collective-permute-done.2.west_ref = bf16[4,512,128]{2,1,0:T(8,128)(2,1)S(1)} collective-permute-done((bf16[4,512,128]{2,1,0:T(8,128)(2,1)S(1)}, bf16[4,512,128]{2,1,0:T(8,128)(2,1)S(1)}, u32[]{:S(2)}, u32[]{:S(2)}) %collective-permute-start.2) | collective-permute-done | bytes 524320 | tf_op jit(solution)/shard_map/ppermute | solution.py:328
  35.3 0.0 copy-start.4
  35.3 2.0 %collective-permute-done.3.east_ref = bf16[4,512,128]{2,1,0:T(8,128)(2,1)} collective-permute-done((bf16[4,512,128]{2,1,0:T(8,128)(2,1)S(1)}, bf16[4,512,128]{2,1,0:T(8,128)(2,1)}, u32[]{:S(2)}, u32[]{:S(2)}) %collective-permute-start.3) | collective-permute-done | bytes 524320 | tf_op jit(solution)/shard_map/ppermute | solution.py:328
  37.4 0.0 copy-done.2
  37.4 0.0 copy-done.3
  37.4 0.0 copy-done
  37.4 0.0 copy-done.4
  37.4 12.8 %shard_map.57 = (f32[4,512,256]{2,1,0:T(8,128)}, bf16[4,512,128]{2,1,0:T(8,128)(2,1)}, bf16[4,512,128]{2,1,0:T(8,128)(2,1)}) custom-call(s32[8,3]{1,0:T(8,128)} %bitcast.1, f32[4,256,256]{2,1,0:T(8,128)} %own_hbm.1, bf16[4,128,256]{2,1,0:T(8,128)(2,1)} %copy-done.2, bf16[4,128,256]{2,1,0:T(8,128)(2,1)} %copy-done.3, bf16[4,512,128]{2,1,0:T(8,128)(2,1)} %copy-done.4, ...), custom_call_target="tpu_custom_call" | custom-call | tf_op jit(solution)/shard_map/pallas_call | solution.py:239
  50.2 10.0 %collective-permute-start.4 = (bf16[4,512,128]{2,1,0:T(8,128)(2,1)}, bf16[4,512,128]{2,1,0:T(8,128)(2,1)S(1)}, u32[]{:S(2)}, u32[]{:S(2)}) collective-permute-start(bf16[4,512,128]{2,1,0:T(8,128)(2,1)} %get-tuple-element.17), channel_id=1, source_target_pairs={{0,1},{1,2},{2,3},{3,4},{4,5},{5,6},{6,7},{8,9},{9,10},{10,11},{11... | collective-permute-start | bytes 1572872 | tf_op jit(solution)/shard_map/ppermute | solution.py:328
  60.2 0.0 copy-start.1
  60.2 2.1 %collective-permute-start.5 = (bf16[4,512,128]{2,1,0:T(8,128)(2,1)}, bf16[4,512,128]{2,1,0:T(8,128)(2,1)S(1)}, u32[]{:S(2)}, u32[]{:S(2)}) collective-permute-start(bf16[4,512,128]{2,1,0:T(8,128)(2,1)} %get-tuple-element.18), channel_id=1, source_target_pairs={{1,0},{2,1},{3,2},{4,3},{5,4},{6,5},{7,6},{9,8},{10,9},{11,10},{12... | collective-permute-start | bytes 1572872 | tf_op jit(solution)/shard_map/ppermute | solution.py:328
  62.2 4.3 %collective-permute-done.4 = bf16[4,512,128]{2,1,0:T(8,128)(2,1)S(1)} collective-permute-done((bf16[4,512,128]{2,1,0:T(8,128)(2,1)}, bf16[4,512,128]{2,1,0:T(8,128)(2,1)S(1)}, u32[]{:S(2)}, u32[]{:S(2)}) %collective-permute-start.4) | collective-permute-done | bytes 524320 | tf_op jit(solution)/shard_map/ppermute | solution.py:328
  66.6 4.4 %collective-permute-done.5 = bf16[4,512,128]{2,1,0:T(8,128)(2,1)S(1)} collective-permute-done((bf16[4,512,128]{2,1,0:T(8,128)(2,1)}, bf16[4,512,128]{2,1,0:T(8,128)(2,1)S(1)}, u32[]{:S(2)}, u32[]{:S(2)}) %collective-permute-start.5) | collective-permute-done | bytes 524320 | tf_op jit(solution)/shard_map/ppermute | solution.py:328
  71.0 1.3 %add_convert_fusion.1 = (bf16[4,128,256]{2,1,0:T(8,128)(2,1)S(1)}, bf16[4,128,256]{2,1,0:T(8,128)(2,1)S(1)}) fusion(f32[4,512,256]{2,1,0:T(8,128)} %get-tuple-element.16, bf16[4,128,128]{2,1,0:T(8,128)(2,1)S(1)} %get-tuple-element.23, bf16[4,128,128]{2,1,0:T(8,128)(2,1)S(1)} %get-tuple-element.21, bf16[4,128,128]{2,1,0:T(8,128)(2,1)S(1)} %get-tuple-element.24, ...), kind=kLoop, calls=%fused_computation.4 | loop fusion | flops 1572864 | bytes 2097152 | tf_op jit(solution)/shard_map/convert_element_type | solution.py:362
  72.4 18.6 %collective-permute-start.6 = (bf16[4,128,256]{2,1,0:T(8,128)(2,1)S(1)}, bf16[4,128,256]{2,1,0:T(8,128)(2,1)S(1)}, u32[]{:S(2)}, u32[]{:S(2)}) collective-permute-start(bf16[4,128,256]{2,1,0:T(8,128)(2,1)S(1)} %get-tuple-element.19), channel_id=1, source_target_pairs={{0,8},{8,16},{16,24},{24,32},{32,40},{40,48},{48,56},{56,64},{64,7... | collective-permute-start | bytes 786440 | tf_op jit(solution)/shard_map/ppermute | solution.py:328
  91.0 1.9 %collective-permute-start.7 = (bf16[4,128,256]{2,1,0:T(8,128)(2,1)S(1)}, bf16[4,128,256]{2,1,0:T(8,128)(2,1)S(1)}, u32[]{:S(2)}, u32[]{:S(2)}) collective-permute-start(bf16[4,128,256]{2,1,0:T(8,128)(2,1)S(1)} %get-tuple-element.20), channel_id=1, source_target_pairs={{8,0},{16,8},{24,16},{32,24},{40,32},{48,40},{56,48},{64,56},{72,6... | collective-permute-start | bytes 786440 | tf_op jit(solution)/shard_map/ppermute | solution.py:328
  93.0 1.3 %collective-permute-done.6 = bf16[4,128,256]{2,1,0:T(8,128)(2,1)S(1)} collective-permute-done((bf16[4,128,256]{2,1,0:T(8,128)(2,1)S(1)}, bf16[4,128,256]{2,1,0:T(8,128)(2,1)S(1)}, u32[]{:S(2)}, u32[]{:S(2)}) %collective-permute-start.6) | collective-permute-done | bytes 262176 | tf_op jit(solution)/shard_map/ppermute | solution.py:328
  94.3 5.9 %collective-permute-done.7 = bf16[4,128,256]{2,1,0:T(8,128)(2,1)S(1)} collective-permute-done((bf16[4,128,256]{2,1,0:T(8,128)(2,1)S(1)}, bf16[4,128,256]{2,1,0:T(8,128)(2,1)S(1)}, u32[]{:S(2)}, u32[]{:S(2)}) %collective-permute-start.7) | collective-permute-done | bytes 262176 | tf_op jit(solution)/shard_map/ppermute | solution.py:328
  100.2 0.0 copy-done.1
  100.2 1.1 %convert_add_fusion = f32[4,256,256]{2,1,0:T(8,128)} fusion(f32[4,512,256]{2,1,0:T(8,128)S(1)} %copy-done.1, bf16[4,256,128]{2,1,0:T(8,128)(2,1)S(1)} %slice.62, bf16[4,256,128]{2,1,0:T(8,128)(2,1)S(1)} %slice.61, bf16[4,128,256]{2,1,0:T(8,128)(2,1)S(1)} %collective-permute-done.7, bf16[4,128,256]{2,1,0:T(8,128)(2,1)S(1)} %collective-permute-done.6), kind=kLoop, calls=%fused_computation | loop fusion | flops 2621440 | bytes 3145728 | tf_op jit(solution)/shard_map/add | solution.py:364
  (8 shorter events, 0.2 us)
Async XLA Ops:
  3.3 13.9 %collective-permute-start = (bf16[4,128,256]{2,1,0:T(8,128)(2,1)}, bf16[4,128,256]{2,1,0:T(8,128)(2,1)S(1)}, u32[]{:S(2)}, u32[]{:S(2)}) collective-permute-start(bf16[4,128,256]{2,1,0:T(8,128)(2,1)} %get-tuple-element.12), channel_id=1, source_target_pairs={{0,8},{8,16},{16,24},{24,32},{32,40},{40,48},{48,56},{56,64},{64,7... | collective-permute-start | bytes 786440 | tf_op jit(solution)/shard_map/ppermute | solution.py:328
  6.1 11.3 %copy-start.6 = (bf16[4,256,128]{2,1,0:T(8,128)(2,1)S(1)}, bf16[4,256,128]{2,1,0:T(8,128)(2,1)}, u32[]{:S(2)}) copy-start(bf16[4,256,128]{2,1,0:T(8,128)(2,1)} %get-tuple-element.14) | copy-start | bytes 786436
  6.1 11.2 %collective-permute-start.1 = (bf16[4,128,256]{2,1,0:T(8,128)(2,1)}, bf16[4,128,256]{2,1,0:T(8,128)(2,1)S(1)}, u32[]{:S(2)}, u32[]{:S(2)}) collective-permute-start(bf16[4,128,256]{2,1,0:T(8,128)(2,1)} %get-tuple-element.13), channel_id=1, source_target_pairs={{8,0},{16,8},{24,16},{32,24},{40,32},{48,40},{56,48},{64,56},{72,6... | collective-permute-start | bytes 786440 | tf_op jit(solution)/shard_map/ppermute | solution.py:328
  10.8 11.9 %copy-start.5 = (bf16[4,256,128]{2,1,0:T(8,128)(2,1)S(1)}, bf16[4,256,128]{2,1,0:T(8,128)(2,1)}, u32[]{:S(2)}) copy-start(bf16[4,256,128]{2,1,0:T(8,128)(2,1)} %get-tuple-element.15) | copy-start | bytes 786436
  10.8 21.2 %all-to-all-start = ((bf16[8,272,256]{2,1,0:T(8,128)(2,1)}), bf16[8,272,256]{2,1,0:T(8,128)(2,1)S(1)}, u32[]{:S(2)}, u32[]{:S(2)}) async-start(bf16[8,272,256]{2,1,0:T(8,128)(2,1)} %shard_map.55), calls=%async_computation | async-start | bytes 2228224 | tf_op jit(solution)/shard_map/all_to_all | solution.py:343
  17.3 20.1 %copy-start.2 = (bf16[4,128,256]{2,1,0:T(8,128)(2,1)}, bf16[4,128,256]{2,1,0:T(8,128)(2,1)S(1)}, u32[]{:S(2)}) copy-start(bf16[4,128,256]{2,1,0:T(8,128)(2,1)S(1)} %collective-permute-done.up_ref) | copy-start | bytes 786436
  17.3 20.0 %copy-start.3 = (bf16[4,128,256]{2,1,0:T(8,128)(2,1)}, bf16[4,128,256]{2,1,0:T(8,128)(2,1)S(1)}, u32[]{:S(2)}) copy-start(bf16[4,128,256]{2,1,0:T(8,128)(2,1)S(1)} %collective-permute-done.1.down_ref) | copy-start | bytes 786436
  17.5 17.9 %collective-permute-start.2 = (bf16[4,512,128]{2,1,0:T(8,128)(2,1)S(1)}, bf16[4,512,128]{2,1,0:T(8,128)(2,1)S(1)}, u32[]{:S(2)}, u32[]{:S(2)}) collective-permute-start(bf16[4,512,128]{2,1,0:T(8,128)(2,1)S(1)} %pad_maximum_fusion), channel_id=1, source_target_pairs={{0,1},{1,2},{2,3},{3,4},{4,5},{5,6},{6,7},{8,9},{9,10},{10,11},{11... | collective-permute-start | bytes 1572872 | tf_op jit(solution)/shard_map/ppermute | solution.py:328
  22.8 14.6 %collective-permute-start.3 = (bf16[4,512,128]{2,1,0:T(8,128)(2,1)S(1)}, bf16[4,512,128]{2,1,0:T(8,128)(2,1)}, u32[]{:S(2)}, u32[]{:S(2)}) collective-permute-start(bf16[4,512,128]{2,1,0:T(8,128)(2,1)S(1)} %pad_maximum_fusion.1), channel_id=1, source_target_pairs={{1,0},{2,1},{3,2},{4,3},{5,4},{6,5},{7,6},{9,8},{10,9},{11,10},{12... | collective-permute-start | bytes 1572872 | tf_op jit(solution)/shard_map/ppermute | solution.py:328
  32.0 5.4 %copy-start = (bf16[8,272,256]{2,1,0:T(8,128)(2,1)}, bf16[8,272,256]{2,1,0:T(8,128)(2,1)S(1)}, u32[]{:S(2)}) copy-start(bf16[8,272,256]{2,1,0:T(8,128)(2,1)S(1)} %all-to-all-done.pat_hbm) | copy-start | bytes 3342340
  35.3 2.0 %copy-start.4 = (bf16[4,512,128]{2,1,0:T(8,128)(2,1)}, bf16[4,512,128]{2,1,0:T(8,128)(2,1)S(1)}, u32[]{:S(2)}) copy-start(bf16[4,512,128]{2,1,0:T(8,128)(2,1)S(1)} %collective-permute-done.2.west_ref) | copy-start | bytes 1572868
  50.2 16.4 %collective-permute-start.4 = (bf16[4,512,128]{2,1,0:T(8,128)(2,1)}, bf16[4,512,128]{2,1,0:T(8,128)(2,1)S(1)}, u32[]{:S(2)}, u32[]{:S(2)}) collective-permute-start(bf16[4,512,128]{2,1,0:T(8,128)(2,1)} %get-tuple-element.17), channel_id=1, source_target_pairs={{0,1},{1,2},{2,3},{3,4},{4,5},{5,6},{6,7},{8,9},{9,10},{10,11},{11... | collective-permute-start | bytes 1572872 | tf_op jit(solution)/shard_map/ppermute | solution.py:328
  60.2 40.1 %copy-start.1 = (f32[4,512,256]{2,1,0:T(8,128)S(1)}, f32[4,512,256]{2,1,0:T(8,128)}, u32[]{:S(2)}) copy-start(f32[4,512,256]{2,1,0:T(8,128)} %get-tuple-element.16) | copy-start | bytes 6291460
  60.2 10.8 %collective-permute-start.5 = (bf16[4,512,128]{2,1,0:T(8,128)(2,1)}, bf16[4,512,128]{2,1,0:T(8,128)(2,1)S(1)}, u32[]{:S(2)}, u32[]{:S(2)}) collective-permute-start(bf16[4,512,128]{2,1,0:T(8,128)(2,1)} %get-tuple-element.18), channel_id=1, source_target_pairs={{1,0},{2,1},{3,2},{4,3},{5,4},{6,5},{7,6},{9,8},{10,9},{11,10},{12... | collective-permute-start | bytes 1572872 | tf_op jit(solution)/shard_map/ppermute | solution.py:328
  72.4 21.9 %collective-permute-start.6 = (bf16[4,128,256]{2,1,0:T(8,128)(2,1)S(1)}, bf16[4,128,256]{2,1,0:T(8,128)(2,1)S(1)}, u32[]{:S(2)}, u32[]{:S(2)}) collective-permute-start(bf16[4,128,256]{2,1,0:T(8,128)(2,1)S(1)} %get-tuple-element.19), channel_id=1, source_target_pairs={{0,8},{8,16},{16,24},{24,32},{32,40},{40,48},{48,56},{56,64},{64,7... | collective-permute-start | bytes 786440 | tf_op jit(solution)/shard_map/ppermute | solution.py:328
  91.0 9.2 %collective-permute-start.7 = (bf16[4,128,256]{2,1,0:T(8,128)(2,1)S(1)}, bf16[4,128,256]{2,1,0:T(8,128)(2,1)S(1)}, u32[]{:S(2)}, u32[]{:S(2)}) collective-permute-start(bf16[4,128,256]{2,1,0:T(8,128)(2,1)S(1)} %get-tuple-element.20), channel_id=1, source_target_pairs={{8,0},{16,8},{24,16},{32,24},{40,32},{48,40},{56,48},{64,56},{72,6... | collective-permute-start | bytes 786440 | tf_op jit(solution)/shard_map/ppermute | solution.py:328
where the time goes:
time: 102 us; the launch traced here: 101 us
  starting transfers between devices  51.6 us (51%)
  waiting for transfers between devices  28 us (27%)
  Pallas kernels  18.2 us (18%)
  other arithmetic  3.16 us (3%)
    ppermute x8, starting transfers between devices, shift(): return lax.ppermute(cells, axis, pairs)  45.2 us
    ppermute x8, waiting for transfers between devices, shift(): return lax.ppermute(cells, axis, pairs)  20.7 us
    pallas_call x1, Pallas kernels, run_windows(): pl.pallas_call(functools.partial(windows_kernel, half), out_shape=(jax.Sh...  12.8 us
    all_to_all x1, waiting for transfers between devices, per_device(): got = lax.all_to_all(sent, 'tx', split_axis=0, concat_axis=0, tiled=True)  7.3 us
    all_to_all x1, starting transfers between devices, per_device(): got = lax.all_to_all(sent, 'tx', split_axis=0, concat_axis=0, tiled=True)  6.42 us
    pallas_call x1, Pallas kernels, edges(): pl.pallas_call(edges_kernel, grid=(slices,), out_shape=(flat, flat, tall,...  3.32 us
    pallas_call x1, Pallas kernels, parcels(): pl.pallas_call(parcel_kernel, out_shape=jax.ShapeDtypeStruct((slots, widt...  2.08 us
  transfers between devices with their start and end apart: 9, of which 7 were waited for; matrix products, arithmetic and copies ran while one was open for 1% of the time, Pallas kernels for 2%

commit v1 on v0

--- a/solution.py
+++ b/solution.py
@@ -21,11 +21,10 @@
     nodes = np.cos((np.arange(512) + 0.5) * np.pi / 512)
     u = 0.5 * (nodes + 1.0)
     v = np.sqrt(u) * limit
-    t = 0.5 * v
-    sinc = np.where(t == 0, 0.5, np.sin(t) / np.where(v == 0, 1.0, v))
+    t = 0.25 * v
     scale = limit * limit
-    a = np.polynomial.polynomial.polyfit(u, sinc, 6) / scale ** np.arange(7)
-    b = np.polynomial.polynomial.polyfit(u, np.cos(t), 7) / scale ** np.arange(8)
+    a = np.polynomial.polynomial.polyfit(u, 2 * np.sin(t) / v, 5) / scale ** np.arange(6)
+    b = np.polynomial.polynomial.polyfit(u, np.cos(t), 5) / scale ** np.arange(6)
     return [float(np.float32(x)) for x in a], [float(np.float32(x)) for x in b]
 
 
@@ -40,7 +39,8 @@
     c = COS_COEFS[-1]
     for b in COS_COEFS[-2::-1]:
         c = c * u + b
-    return s * v, c
+    s = s * v
+    return s * c, 1.0 - 0.5 * (s * s)
 
 
 def make_tables(length):
@@ -65,15 +65,16 @@
 
 
 def windows_kernel(
-    half, where_ref, own_hbm, up_ref, down_ref, west_ref, east_ref, probe_hbm, pat_hbm, tab_hbm,
-    mid_ref, wout_ref, eout_ref,
-    ext_ref, acc_ref, order_ref, own_ref, probe_ref, pat_ref, tab_ref, sems, *streams,
+    half, where_ref, own_hbm, up_hbm, down_hbm, west_hbm, east_hbm, probe_hbm, pat_hbm, tab_hbm,
+    mid_hbm, wout_hbm, eout_hbm,
+    ext_ref, acc_ref, order_ref, own_ref, up_ref, down_ref, west_ref, east_ref, probe_ref, pat_ref,
+    tab_ref, mid_ref, wout_ref, eout_ref, in_sems, out_sems, *streams,
 ):
+    sources = (west_hbm, east_hbm, up_hbm, down_hbm, own_hbm, tab_hbm, probe_hbm, pat_hbm)
+    targets = (west_ref, east_ref, up_ref, down_ref, own_ref, tab_ref, probe_ref, pat_ref)
     loads = [
-        pltpu.make_async_copy(own_hbm, own_ref, sems.at[0]),
-        pltpu.make_async_copy(tab_hbm, tab_ref, sems.at[1]),
-        pltpu.make_async_copy(probe_hbm, probe_ref, sems.at[2]),
-        pltpu.make_async_copy(pat_hbm, pat_ref, sems.at[3]),
+        pltpu.make_async_copy(source, into, in_sems.at[i])
+        for i, (source, into) in enumerate(zip(sources, targets))
     ]
     for load in loads:
         load.start()
@@ -91,21 +92,23 @@
         return pl.ds(start * PITCH + block, count, stride=PITCH)
 
     for s in range(slices):
+        acc_ref[s] = jnp.zeros(acc_ref.shape[1:], f32)
+    for load in loads[:2]:
+        load.wait()
+    for s in range(slices):
         for c in range(side):
             lanes = slice(c * LANES, (c + 1) * LANES)
             ext_ref[s, every(0, tall, c)] = west_ref[s, :, lanes].astype(f32)
             ext_ref[s, every(0, tall, blocks - side + c)] = east_ref[s, :, lanes].astype(f32)
+    for load in loads[2:5]:
+        load.wait()
+    for s in range(slices):
         for c in range(blocks - 2 * side):
             lanes = slice(c * LANES, (c + 1) * LANES)
             ext_ref[s, every(0, half, side + c)] = up_ref[s, :, lanes].astype(f32)
             ext_ref[s, every(half + tile_y, half, side + c)] = down_ref[s, :, lanes].astype(f32)
-        acc_ref[s] = jnp.zeros(acc_ref.shape[1:], f32)
-    loads[0].wait()
-    for s in range(slices):
-        for c in range(blocks - 2 * side):
-            inner = own_ref[s, :, c * LANES : (c + 1) * LANES].astype(bf16).astype(f32)
-            ext_ref[s, every(half, tile_y, side + c)] = inner
-    for load in loads[1:]:
+            ext_ref[s, every(half, tile_y, side + c)] = own_ref[s, :, lanes].astype(bf16).astype(f32)
+    for load in loads[5:]:
         load.wait()
 
     def dot(a, b):
@@ -215,6 +218,7 @@
         for _ in one_window(order_ref[filled - 1], *streams[:4]):
             pass
 
+    stores = []
     for s in range(slices):
         for b in range(blocks):
             part = acc_ref[s, every(0, tall, b)]
@@ -226,6 +230,13 @@
             else:
                 c = b - side
                 mid_ref[s, :, c * LANES : (c + 1) * LANES] = part
+        for j, (source, into) in enumerate(
+            ((mid_ref, mid_hbm), (wout_ref, wout_hbm), (eout_ref, eout_hbm))
+        ):
+            stores.append(pltpu.make_async_copy(source.at[s], into.at[s], out_sems.at[s, j]))
+            stores[-1].start()
+    for store in stores:
+        store.wait()
 
 
 def run_windows(where, own, up, down, west, east, probe, patterns, tables, interpret=False):
@@ -234,7 +245,6 @@
     half = width // 2
     tall = tile_y + width
     f32, bf16 = jnp.float32, jnp.bfloat16
-    vmem = pl.BlockSpec(memory_space=pltpu.VMEM)
     hbm = pl.BlockSpec(memory_space=pltpu.HBM)
     return pl.pallas_call(
         functools.partial(windows_kernel, half),
@@ -243,17 +253,23 @@
             jax.ShapeDtypeStruct((slices, tall, half), bf16),
             jax.ShapeDtypeStruct((slices, tall, half), bf16),
         ),
-        in_specs=[pl.BlockSpec(memory_space=pltpu.SMEM), hbm] + [vmem] * 4 + [hbm] * 3,
-        out_specs=(vmem,) * 3,
+        in_specs=[pl.BlockSpec(memory_space=pltpu.SMEM)] + [hbm] * 8,
+        out_specs=(hbm,) * 3,
         scratch_shapes=[
             pltpu.VMEM((slices, tall * PITCH, LANES), f32),
             pltpu.VMEM((slices, tall * PITCH, LANES), f32),
             pltpu.SMEM((patterns.shape[0] + 1,), jnp.int32),
-            pltpu.VMEM(own.shape, f32),
-            pltpu.VMEM(probe.shape, f32),
-            pltpu.VMEM(patterns.shape, bf16),
-            pltpu.VMEM(tables.shape, bf16),
-            pltpu.SemaphoreType.DMA((4,)),
+        ]
+        + [
+            pltpu.VMEM(x.shape, x.dtype)
+            for x in (own, up, down, west, east, probe, patterns, tables)
+        ]
+        + [
+            pltpu.VMEM((slices, tall, tile_x), f32),
+            pltpu.VMEM((slices, tall, half), bf16),
+            pltpu.VMEM((slices, tall, half), bf16),
+            pltpu.SemaphoreType.DMA((8,)),
+            pltpu.SemaphoreType.DMA((slices, 3)),
         ]
         + [
             pltpu.VMEM((slices, 2, width, width), f32),
@@ -267,57 +283,42 @@
     )(where, own, up, down, west, east, probe, patterns, tables)
 
 
-def edges_kernel(own_ref, up_ref, down_ref, west_ref, east_ref):
-    half = up_ref.shape[1]
-    tile_y, tile_x = own_ref.shape[1:]
-    bf16 = jnp.bfloat16
-    up_ref[...] = own_ref[:, :half].astype(bf16)
-    down_ref[...] = own_ref[:, tile_y - half :].astype(bf16)
-    west_ref[...] = own_ref[:, :, :half].astype(bf16)
-    east_ref[...] = own_ref[:, :, tile_x - half :].astype(bf16)
-
-
-def edges(own, half):
-    slices, tile_y, tile_x = own.shape
-    bf16 = jnp.bfloat16
-    flat = jax.ShapeDtypeStruct((slices, half, tile_x), bf16)
-    tall = jax.ShapeDtypeStruct((slices, tile_y, half), bf16)
-
-    def slab(shape):
-        return pl.BlockSpec((1,) + shape[1:], lambda s: (s, 0, 0))
-
-    return pl.pallas_call(
-        edges_kernel,
-        grid=(slices,),
-        out_shape=(flat, flat, tall, tall),
-        in_specs=[slab(own.shape)],
-        out_specs=tuple(slab(x.shape) for x in (flat, flat, tall, tall)),
-        compiler_params=pltpu.CompilerParams(vmem_limit_bytes=56 << 20),
-    )(own)
-
-
-def parcel_kernel(centers_ref, pat_ref, sent_ref):
-    slots, _, width = sent_ref.shape
-    bf16 = jnp.bfloat16
-    lane = lax.broadcasted_iota(jnp.int32, (SLOT_PAD, width), 1)
-    sent_ref[...] = jnp.zeros(sent_ref.shape, bf16)
-    for p in range(pat_ref.shape[0]):
-        owner = centers_ref[p, 1] // TILE
+def parcel_kernel(centers_ref, pat_hbm, sent_hbm, info_ref, sems):
+    count, width, _ = pat_hbm.shape
+    owners = [centers_ref[p, 1] // TILE for p in range(count)]
+    copies = [
+        pltpu.make_async_copy(pat_hbm.at[p], sent_hbm.at[owners[p], pl.ds(0, width)], sems.at[p])
+        for p in range(count)
+    ]
+    for copy in copies:
+        copy.start()
+    lane = lax.broadcasted_iota(jnp.int32, info_ref.shape[1:], 1)
+    info_ref[...] = jnp.zeros(info_ref.shape, jnp.bfloat16)
+    for p in range(count):
         row = centers_ref[p, 0] % TILE
         col = centers_ref[p, 1] % TILE
         info = jnp.where(lane == 0, row, jnp.where(lane == 1, col, jnp.where(lane == 2, 1, 0)))
-        sent_ref[owner, :width] = pat_ref[p]
-        sent_ref[owner, width:] = info.astype(jnp.float32).astype(bf16)
+        info_ref[owners[p]] = info.astype(jnp.float32).astype(jnp.bfloat16)
+    copies.append(
+        pltpu.make_async_copy(info_ref, sent_hbm.at[:, pl.ds(width, SLOT_PAD)], sems.at[count])
+    )
+    copies[-1].start()
+    for copy in copies:
+        copy.wait()
 
 
 def parcels(centers, patterns, slots):
-    width = patterns.shape[1]
-    vmem = pl.BlockSpec(memory_space=pltpu.VMEM)
+    count, width, _ = patterns.shape
+    hbm = pl.BlockSpec(memory_space=pltpu.HBM)
     return pl.pallas_call(
         parcel_kernel,
         out_shape=jax.ShapeDtypeStruct((slots, width + SLOT_PAD, width), jnp.bfloat16),
-        in_specs=[pl.BlockSpec(memory_space=pltpu.SMEM), vmem],
-        out_specs=vmem,
+        in_specs=[pl.BlockSpec(memory_space=pltpu.SMEM), hbm],
+        out_specs=hbm,
+        scratch_shapes=[
+            pltpu.VMEM((slots, SLOT_PAD, width), jnp.bfloat16),
+            pltpu.SemaphoreType.DMA((count + 1,)),
+        ],
         compiler_params=pltpu.CompilerParams(vmem_limit_bytes=56 << 20),
     )(centers, patterns)
 
@@ -335,18 +336,19 @@
     columns = lax.axis_size("tx")
     f32, bf16 = jnp.float32, jnp.bfloat16
 
-    first_rows, last_rows, first_cols, last_cols = edges(potential, half)
-    up = shift(last_rows, "ty", 1)
-    down = shift(first_rows, "ty", -1)
+    rounded = potential.astype(bf16)
+    up = shift(rounded[:, tile_y - half :], "ty", 1)
+    down = shift(rounded[:, :half], "ty", -1)
 
     sent = parcels(scan_centers, patterns, columns)
     got = lax.all_to_all(sent, "tx", split_axis=0, concat_axis=0, tiled=True)
     where = got[:, width, :3].astype(f32).astype(jnp.int32)
 
-    west = shift(
-        jnp.concatenate([up[:, :, tile_x - half :], last_cols, down[:, :, tile_x - half :]], 1), "tx", 1
-    )
-    east = shift(jnp.concatenate([up[:, :, :half], first_cols, down[:, :, :half]], 1), "tx", -1)
+    def strip(cols):
+        return jnp.concatenate([up[:, :, cols], rounded[:, :, cols], down[:, :, cols]], 1)
+
+    west = shift(strip(slice(tile_x - half, tile_x)), "tx", 1)
+    east = shift(strip(slice(0, half)), "tx", -1)
 
     mid, to_west, to_east = run_windows(
         where, potential, up, down, west, east, probe, got, tables

time: 102 us -> 106 us (1.039)
  the two profiles are of different devices: /device:TPU:57 before, /device:TPU:29 now
where the time goes in v1:
time: 106 us; the launch traced here: 104 us
  Pallas kernels  42 us (40%)
  starting transfers between devices  29.2 us (28%)
  waiting for transfers between devices  28.1 us (27%)
  other arithmetic  4.44 us (4%)
    pallas_call x1, Pallas kernels, run_windows(): pl.pallas_call(functools.partial(windows_kernel, half), out_shape=(jax.Sh...  32.2 us
    ppermute x8, starting transfers between devices, shift(): return lax.ppermute(cells, axis, pairs)  22.6 us
    ppermute x8, waiting for transfers between devices, shift(): return lax.ppermute(cells, axis, pairs)  18.1 us
    all_to_all x1, waiting for transfers between devices, per_device(): got = lax.all_to_all(sent, 'tx', split_axis=0, concat_axis=0, tiled=True)  9.98 us
    pallas_call x1, Pallas kernels, parcels(): pl.pallas_call(parcel_kernel, out_shape=jax.ShapeDtypeStruct((slots, widt...  9.77 us
    all_to_all x1, starting transfers between devices, per_device(): got = lax.all_to_all(sent, 'tx', split_axis=0, concat_axis=0, tiled=True)  6.56 us
  transfers between devices with their start and end apart: 9, of which 7 were waited for; matrix products, arithmetic and copies ran while one was open for 1% of the time, Pallas kernels for 9%

profile of v1, /device:TPU:29, one launch (start us, length us, event | category | flops | bytes accessed | tf_op | source)
XLA Modules:
  0.0 104.2 jit_solution(11487267743471728278)
XLA Ops:
  0.0 1.3 %convert_element_type.33 = bf16[4,256,256]{2,1,0:T(8,128)(2,1)S(1)} convert(f32[4,256,256]{2,1,0:T(8,128)} %own_hbm.1) | non-fusion elementwise | flops 262144 | bytes 1572864 | tf_op jit(solution)/shard_map/convert_element_type | solution.py:339
  1.3 2.4 %collective-permute-start.1 = (bf16[4,128,256]{2,1,0:T(8,128)(2,1)S(1)}, bf16[4,128,256]{2,1,0:T(8,128)(2,1)S(1)}, u32[]{:S(2)}, u32[]{:S(2)}) collective-permute-start(bf16[4,128,256]{2,1,0:T(8,128)(2,1)S(1)} %get-tuple-element.19), channel_id=1, source_target_pairs={{8,0},{16,8},{24,16},{32,24},{40,32},{48,40},{56,48},{64,56},{72,6... | collective-permute-start | bytes 786440 | tf_op jit(solution)/shard_map/ppermute | solution.py:329
  3.7 5.0 %collective-permute-start = (bf16[4,128,256]{2,1,0:T(8,128)(2,1)S(1)}, bf16[4,128,256]{2,1,0:T(8,128)(2,1)S(1)}, u32[]{:S(2)}, u32[]{:S(2)}) collective-permute-start(bf16[4,128,256]{2,1,0:T(8,128)(2,1)S(1)} %get-tuple-element.20), channel_id=1, source_target_pairs={{0,8},{8,16},{16,24},{24,32},{32,40},{40,48},{48,56},{56,64},{64,7... | collective-permute-start | bytes 786440 | tf_op jit(solution)/shard_map/ppermute | solution.py:329
  8.7 9.8 %shard_map.55 = bf16[8,272,256]{2,1,0:T(8,128)(2,1)} custom-call(s32[2,2]{1,0:T(2,128)} %centers_ref.1, bf16[2,256,256]{2,1,0:T(8,128)(2,1)} %pat_hbm.1), custom_call_target="tpu_custom_call" | custom-call | tf_op jit(solution)/shard_map/pallas_call | solution.py:313
  18.5 6.6 %all-to-all-start = ((bf16[8,272,256]{2,1,0:T(8,128)(2,1)}), bf16[8,272,256]{2,1,0:T(8,128)(2,1)S(1)}, u32[]{:S(2)}, u32[]{:S(2)}) async-start(bf16[8,272,256]{2,1,0:T(8,128)(2,1)} %shard_map.55), calls=%async_computation | async-start | bytes 2228224 | tf_op jit(solution)/shard_map/all_to_all | solution.py:344
  25.1 0.1 fusion.3
  25.2 0.0 collective-permute-done.1.down_hbm
  25.2 0.0 copy-start.2
  25.2 0.0 collective-permute-done.up_hbm
  25.3 0.0 copy-start.3
  25.4 3.5 %collective-permute-start.2 = (bf16[4,512,128]{2,1,0:T(8,128)(2,1)S(1)}, bf16[4,512,128]{2,1,0:T(8,128)(2,1)S(1)}, u32[]{:S(2)}, u32[]{:S(2)}) collective-permute-start(bf16[4,512,128]{2,1,0:T(8,128)(2,1)S(1)} %pad_maximum_fusion), channel_id=1, source_target_pairs={{0,1},{1,2},{2,3},{3,4},{4,5},{5,6},{6,7},{8,9},{9,10},{10,11},{11... | collective-permute-start | bytes 1572872 | tf_op jit(solution)/shard_map/ppermute | solution.py:329
  29.0 1.9 %collective-permute-start.3 = (bf16[4,512,128]{2,1,0:T(8,128)(2,1)S(1)}, bf16[4,512,128]{2,1,0:T(8,128)(2,1)}, u32[]{:S(2)}, u32[]{:S(2)}) collective-permute-start(bf16[4,512,128]{2,1,0:T(8,128)(2,1)S(1)} %pad_maximum_fusion.1), channel_id=1, source_target_pairs={{1,0},{2,1},{3,2},{4,3},{5,4},{6,5},{7,6},{9,8},{10,9},{11,10},{12... | collective-permute-start | bytes 1572872 | tf_op jit(solution)/shard_map/ppermute | solution.py:329
  30.9 10.0 %all-to-all-done.pat_hbm = bf16[8,272,256]{2,1,0:T(8,128)(2,1)S(1)} async-done(((bf16[8,272,256]{2,1,0:T(8,128)(2,1)}), bf16[8,272,256]{2,1,0:T(8,128)(2,1)S(1)}, u32[]{:S(2)}, u32[]{:S(2)}) %all-to-all-start) | async-done | bytes 1114144 | tf_op jit(solution)/shard_map/all_to_all | solution.py:344
  40.9 0.0 copy-start
  40.9 0.6 fusion
  41.5 1.9 %collective-permute-done.2.west_hbm = bf16[4,512,128]{2,1,0:T(8,128)(2,1)S(1)} collective-permute-done((bf16[4,512,128]{2,1,0:T(8,128)(2,1)S(1)}, bf16[4,512,128]{2,1,0:T(8,128)(2,1)S(1)}, u32[]{:S(2)}, u32[]{:S(2)}) %collective-permute-start.2) | collective-permute-done | bytes 524320 | tf_op jit(solution)/shard_map/ppermute | solution.py:329
  43.4 0.0 copy-start.4
  43.4 1.9 %collective-permute-done.3.east_hbm = bf16[4,512,128]{2,1,0:T(8,128)(2,1)} collective-permute-done((bf16[4,512,128]{2,1,0:T(8,128)(2,1)S(1)}, bf16[4,512,128]{2,1,0:T(8,128)(2,1)}, u32[]{:S(2)}, u32[]{:S(2)}) %collective-permute-start.3) | collective-permute-done | bytes 524320 | tf_op jit(solution)/shard_map/ppermute | solution.py:329
  45.3 0.0 copy-done.2
  45.3 0.0 copy-done.3
  45.3 0.0 copy-done
  45.3 0.0 copy-done.4
  45.3 32.2 %shard_map.56 = (f32[4,512,256]{2,1,0:T(8,128)}, bf16[4,512,128]{2,1,0:T(8,128)(2,1)}, bf16[4,512,128]{2,1,0:T(8,128)(2,1)}) custom-call(s32[8,3]{1,0:T(8,128)} %bitcast.1, f32[4,256,256]{2,1,0:T(8,128)} %own_hbm.1, bf16[4,128,256]{2,1,0:T(8,128)(2,1)} %copy-done.3, bf16[4,128,256]{2,1,0:T(8,128)(2,1)} %copy-done.2, bf16[4,512,128]{2,1,0:T(8,128)(2,1)} %copy-done.4, ...), custom_call_target="tpu_custom_call" | custom-call | tf_op jit(solution)/shard_map/pallas_call | solution.py:249
  77.5 1.9 %collective-permute-start.4 = (bf16[4,512,128]{2,1,0:T(8,128)(2,1)}, bf16[4,512,128]{2,1,0:T(8,128)(2,1)S(1)}, u32[]{:S(2)}, u32[]{:S(2)}) collective-permute-start(bf16[4,512,128]{2,1,0:T(8,128)(2,1)} %get-tuple-element.9), channel_id=1, source_target_pairs={{0,1},{1,2},{2,3},{3,4},{4,5},{5,6},{6,7},{8,9},{9,10},{10,11},{11... | collective-permute-start | bytes 1572872 | tf_op jit(solution)/shard_map/ppermute | solution.py:329
  79.4 0.0 copy-start.1
  79.4 2.6 %collective-permute-start.5 = (bf16[4,512,128]{2,1,0:T(8,128)(2,1)}, bf16[4,512,128]{2,1,0:T(8,128)(2,1)S(1)}, u32[]{:S(2)}, u32[]{:S(2)}) collective-permute-start(bf16[4,512,128]{2,1,0:T(8,128)(2,1)} %get-tuple-element.10), channel_id=1, source_target_pairs={{1,0},{2,1},{3,2},{4,3},{5,4},{6,5},{7,6},{9,8},{10,9},{11,10},{12... | collective-permute-start | bytes 1572872 | tf_op jit(solution)/shard_map/ppermute | solution.py:329
  82.0 3.8 %collective-permute-done.4 = bf16[4,512,128]{2,1,0:T(8,128)(2,1)S(1)} collective-permute-done((bf16[4,512,128]{2,1,0:T(8,128)(2,1)}, bf16[4,512,128]{2,1,0:T(8,128)(2,1)S(1)}, u32[]{:S(2)}, u32[]{:S(2)}) %collective-permute-start.4) | collective-permute-done | bytes 524320 | tf_op jit(solution)/shard_map/ppermute | solution.py:329
  85.9 4.7 %collective-permute-done.5 = bf16[4,512,128]{2,1,0:T(8,128)(2,1)S(1)} collective-permute-done((bf16[4,512,128]{2,1,0:T(8,128)(2,1)}, bf16[4,512,128]{2,1,0:T(8,128)(2,1)S(1)}, u32[]{:S(2)}, u32[]{:S(2)}) %collective-permute-start.5) | collective-permute-done | bytes 524320 | tf_op jit(solution)/shard_map/ppermute | solution.py:329
  90.6 1.3 %add_convert_fusion.1 = (bf16[4,128,256]{2,1,0:T(8,128)(2,1)S(1)}, bf16[4,128,256]{2,1,0:T(8,128)(2,1)S(1)}) fusion(f32[4,512,256]{2,1,0:T(8,128)} %get-tuple-element.8, bf16[4,128,128]{2,1,0:T(8,128)(2,1)S(1)} %get-tuple-element.15, bf16[4,128,128]{2,1,0:T(8,128)(2,1)S(1)} %get-tuple-element.13, bf16[4,128,128]{2,1,0:T(8,128)(2,1)S(1)} %get-tuple-element.16, ...), kind=kLoop, calls=%fused_computation.4 | loop fusion | flops 1572864 | bytes 2097152 | tf_op jit(solution)/shard_map/convert_element_type | solution.py:364
  91.9 1.9 %collective-permute-start.6 = (bf16[4,128,256]{2,1,0:T(8,128)(2,1)S(1)}, bf16[4,128,256]{2,1,0:T(8,128)(2,1)S(1)}, u32[]{:S(2)}, u32[]{:S(2)}) collective-permute-start(bf16[4,128,256]{2,1,0:T(8,128)(2,1)S(1)} %get-tuple-element.11), channel_id=1, source_target_pairs={{0,8},{8,16},{16,24},{24,32},{32,40},{40,48},{48,56},{56,64},{64,7... | collective-permute-start | bytes 786440 | tf_op jit(solution)/shard_map/ppermute | solution.py:329
  93.9 3.4 %collective-permute-start.7 = (bf16[4,128,256]{2,1,0:T(8,128)(2,1)S(1)}, bf16[4,128,256]{2,1,0:T(8,128)(2,1)S(1)}, u32[]{:S(2)}, u32[]{:S(2)}) collective-permute-start(bf16[4,128,256]{2,1,0:T(8,128)(2,1)S(1)} %get-tuple-element.12), channel_id=1, source_target_pairs={{8,0},{16,8},{24,16},{32,24},{40,32},{48,40},{56,48},{64,56},{72,6... | collective-permute-start | bytes 786440 | tf_op jit(solution)/shard_map/ppermute | solution.py:329
  97.3 1.8 %collective-permute-done.6 = bf16[4,128,256]{2,1,0:T(8,128)(2,1)S(1)} collective-permute-done((bf16[4,128,256]{2,1,0:T(8,128)(2,1)S(1)}, bf16[4,128,256]{2,1,0:T(8,128)(2,1)S(1)}, u32[]{:S(2)}, u32[]{:S(2)}) %collective-permute-start.6) | collective-permute-done | bytes 262176 | tf_op jit(solution)/shard_map/ppermute | solution.py:329
  99.0 4.0 %collective-permute-done.7 = bf16[4,128,256]{2,1,0:T(8,128)(2,1)S(1)} collective-permute-done((bf16[4,128,256]{2,1,0:T(8,128)(2,1)S(1)}, bf16[4,128,256]{2,1,0:T(8,128)(2,1)S(1)}, u32[]{:S(2)}, u32[]{:S(2)}) %collective-permute-start.7) | collective-permute-done | bytes 262176 | tf_op jit(solution)/shard_map/ppermute | solution.py:329
  103.1 0.0 copy-done.1
  103.1 1.1 %convert_add_fusion = f32[4,256,256]{2,1,0:T(8,128)} fusion(f32[4,512,256]{2,1,0:T(8,128)S(1)} %copy-done.1, bf16[4,256,128]{2,1,0:T(8,128)(2,1)S(1)} %slice.82, bf16[4,256,128]{2,1,0:T(8,128)(2,1)S(1)} %slice.81, bf16[4,128,256]{2,1,0:T(8,128)(2,1)S(1)} %collective-permute-done.7, bf16[4,128,256]{2,1,0:T(8,128)(2,1)S(1)} %collective-permute-done.6), kind=kLoop, calls=%fused_computation | loop fusion | flops 2621440 | bytes 3145728 | tf_op jit(solution)/shard_map/add | solution.py:366
  (9 shorter events, 0.3 us)
Async XLA Ops:
  1.3 23.8 %collective-permute-start.1 = (bf16[4,128,256]{2,1,0:T(8,128)(2,1)S(1)}, bf16[4,128,256]{2,1,0:T(8,128)(2,1)S(1)}, u32[]{:S(2)}, u32[]{:S(2)}) collective-permute-start(bf16[4,128,256]{2,1,0:T(8,128)(2,1)S(1)} %get-tuple-element.19), channel_id=1, source_target_pairs={{8,0},{16,8},{24,16},{32,24},{40,32},{48,40},{56,48},{64,56},{72,6... | collective-permute-start | bytes 786440 | tf_op jit(solution)/shard_map/ppermute | solution.py:329
  3.7 21.5 %collective-permute-start = (bf16[4,128,256]{2,1,0:T(8,128)(2,1)S(1)}, bf16[4,128,256]{2,1,0:T(8,128)(2,1)S(1)}, u32[]{:S(2)}, u32[]{:S(2)}) collective-permute-start(bf16[4,128,256]{2,1,0:T(8,128)(2,1)S(1)} %get-tuple-element.20), channel_id=1, source_target_pairs={{0,8},{8,16},{16,24},{24,32},{32,40},{40,48},{48,56},{56,64},{64,7... | collective-permute-start | bytes 786440 | tf_op jit(solution)/shard_map/ppermute | solution.py:329
  18.5 22.4 %all-to-all-start = ((bf16[8,272,256]{2,1,0:T(8,128)(2,1)}), bf16[8,272,256]{2,1,0:T(8,128)(2,1)S(1)}, u32[]{:S(2)}, u32[]{:S(2)}) async-start(bf16[8,272,256]{2,1,0:T(8,128)(2,1)} %shard_map.55), calls=%async_computation | async-start | bytes 2228224 | tf_op jit(solution)/shard_map/all_to_all | solution.py:344
  25.2 20.1 %copy-start.2 = (bf16[4,128,256]{2,1,0:T(8,128)(2,1)}, bf16[4,128,256]{2,1,0:T(8,128)(2,1)S(1)}, u32[]{:S(2)}) copy-start(bf16[4,128,256]{2,1,0:T(8,128)(2,1)S(1)} %collective-permute-done.1.down_hbm) | copy-start | bytes 786436
  25.3 20.0 %copy-start.3 = (bf16[4,128,256]{2,1,0:T(8,128)(2,1)}, bf16[4,128,256]{2,1,0:T(8,128)(2,1)S(1)}, u32[]{:S(2)}) copy-start(bf16[4,128,256]{2,1,0:T(8,128)(2,1)S(1)} %collective-permute-done.up_hbm) | copy-start | bytes 786436
  25.4 18.0 %collective-permute-start.2 = (bf16[4,512,128]{2,1,0:T(8,128)(2,1)S(1)}, bf16[4,512,128]{2,1,0:T(8,128)(2,1)S(1)}, u32[]{:S(2)}, u32[]{:S(2)}) collective-permute-start(bf16[4,512,128]{2,1,0:T(8,128)(2,1)S(1)} %pad_maximum_fusion), channel_id=1, source_target_pairs={{0,1},{1,2},{2,3},{3,4},{4,5},{5,6},{6,7},{8,9},{9,10},{10,11},{11... | collective-permute-start | bytes 1572872 | tf_op jit(solution)/shard_map/ppermute | solution.py:329
  29.0 16.3 %collective-permute-start.3 = (bf16[4,512,128]{2,1,0:T(8,128)(2,1)S(1)}, bf16[4,512,128]{2,1,0:T(8,128)(2,1)}, u32[]{:S(2)}, u32[]{:S(2)}) collective-permute-start(bf16[4,512,128]{2,1,0:T(8,128)(2,1)S(1)} %pad_maximum_fusion.1), channel_id=1, source_target_pairs={{1,0},{2,1},{3,2},{4,3},{5,4},{6,5},{7,6},{9,8},{10,9},{11,10},{12... | collective-permute-start | bytes 1572872 | tf_op jit(solution)/shard_map/ppermute | solution.py:329
  40.9 4.4 %copy-start = (bf16[8,272,256]{2,1,0:T(8,128)(2,1)}, bf16[8,272,256]{2,1,0:T(8,128)(2,1)S(1)}, u32[]{:S(2)}) copy-start(bf16[8,272,256]{2,1,0:T(8,128)(2,1)S(1)} %all-to-all-done.pat_hbm) | copy-start | bytes 3342340
  43.4 1.9 %copy-start.4 = (bf16[4,512,128]{2,1,0:T(8,128)(2,1)}, bf16[4,512,128]{2,1,0:T(8,128)(2,1)S(1)}, u32[]{:S(2)}) copy-start(bf16[4,512,128]{2,1,0:T(8,128)(2,1)S(1)} %collective-permute-done.2.west_hbm) | copy-start | bytes 1572868
  77.5 8.3 %collective-permute-start.4 = (bf16[4,512,128]{2,1,0:T(8,128)(2,1)}, bf16[4,512,128]{2,1,0:T(8,128)(2,1)S(1)}, u32[]{:S(2)}, u32[]{:S(2)}) collective-permute-start(bf16[4,512,128]{2,1,0:T(8,128)(2,1)} %get-tuple-element.9), channel_id=1, source_target_pairs={{0,1},{1,2},{2,3},{3,4},{4,5},{5,6},{6,7},{8,9},{9,10},{10,11},{11... | collective-permute-start | bytes 1572872 | tf_op jit(solution)/shard_map/ppermute | solution.py:329
  79.4 23.7 %copy-start.1 = (f32[4,512,256]{2,1,0:T(8,128)S(1)}, f32[4,512,256]{2,1,0:T(8,128)}, u32[]{:S(2)}) copy-start(f32[4,512,256]{2,1,0:T(8,128)} %get-tuple-element.8) | copy-start | bytes 6291460
  79.4 11.1 %collective-permute-start.5 = (bf16[4,512,128]{2,1,0:T(8,128)(2,1)}, bf16[4,512,128]{2,1,0:T(8,128)(2,1)S(1)}, u32[]{:S(2)}, u32[]{:S(2)}) collective-permute-start(bf16[4,512,128]{2,1,0:T(8,128)(2,1)} %get-tuple-element.10), channel_id=1, source_target_pairs={{1,0},{2,1},{3,2},{4,3},{5,4},{6,5},{7,6},{9,8},{10,9},{11,10},{12... | collective-permute-start | bytes 1572872 | tf_op jit(solution)/shard_map/ppermute | solution.py:329
  91.9 7.1 %collective-permute-start.6 = (bf16[4,128,256]{2,1,0:T(8,128)(2,1)S(1)}, bf16[4,128,256]{2,1,0:T(8,128)(2,1)S(1)}, u32[]{:S(2)}, u32[]{:S(2)}) collective-permute-start(bf16[4,128,256]{2,1,0:T(8,128)(2,1)S(1)} %get-tuple-element.11), channel_id=1, source_target_pairs={{0,8},{8,16},{16,24},{24,32},{32,40},{40,48},{48,56},{56,64},{64,7... | collective-permute-start | bytes 786440 | tf_op jit(solution)/shard_map/ppermute | solution.py:329
  93.9 9.2 %collective-permute-start.7 = (bf16[4,128,256]{2,1,0:T(8,128)(2,1)S(1)}, bf16[4,128,256]{2,1,0:T(8,128)(2,1)S(1)}, u32[]{:S(2)}, u32[]{:S(2)}) collective-permute-start(bf16[4,128,256]{2,1,0:T(8,128)(2,1)S(1)} %get-tuple-element.12), channel_id=1, source_target_pairs={{8,0},{16,8},{24,16},{32,24},{40,32},{48,40},{56,48},{64,56},{72,6... | collective-permute-start | bytes 786440 | tf_op jit(solution)/shard_map/ppermute | solution.py:329

commit v2 on v1

--- a/solution.py
+++ b/solution.py
@@ -178,16 +178,15 @@
         for k in chunks():
             re, im = z[k, :width], z[k, width:]
             excess = re * re + im * im - pat_ref[slot, k].astype(f32)
-            twice = excess + excess
-            t_ref[k, :width] = (twice * re).astype(bf16)
-            t_ref[k, width:] = (twice * im).astype(bf16)
+            t_ref[k, :width] = (excess * re).astype(bf16)
+            t_ref[k, width:] = (excess * im).astype(bf16)
         for s in range(slices - 1, -1, -1):
             yield
             g = apply_back(2 if s == slices - 1 else 0)
             yield
             for k in chunks():
                 re, im = g[k], g[width + k.start : width + k.stop]
-                grad = 0.5 * (im * phi_ref[s, 0, k] - re * phi_ref[s, 1, k])
+                grad = im * phi_ref[s, 0, k] - re * phi_ref[s, 1, k]
                 deposit(s, k, grad)
                 if s:
                     cos, sin = cs_ref[s, 0, k], cs_ref[s, 1, k]
@@ -283,42 +282,28 @@
     )(where, own, up, down, west, east, probe, patterns, tables)
 
 
-def parcel_kernel(centers_ref, pat_hbm, sent_hbm, info_ref, sems):
-    count, width, _ = pat_hbm.shape
-    owners = [centers_ref[p, 1] // TILE for p in range(count)]
-    copies = [
-        pltpu.make_async_copy(pat_hbm.at[p], sent_hbm.at[owners[p], pl.ds(0, width)], sems.at[p])
-        for p in range(count)
-    ]
-    for copy in copies:
-        copy.start()
-    lane = lax.broadcasted_iota(jnp.int32, info_ref.shape[1:], 1)
-    info_ref[...] = jnp.zeros(info_ref.shape, jnp.bfloat16)
-    for p in range(count):
+def parcel_kernel(centers_ref, pat_ref, sent_ref):
+    slots, _, width = sent_ref.shape
+    bf16 = jnp.bfloat16
+    lane = lax.broadcasted_iota(jnp.int32, (SLOT_PAD, width), 1)
+    sent_ref[...] = jnp.zeros(sent_ref.shape, bf16)
+    for p in range(pat_ref.shape[0]):
+        owner = centers_ref[p, 1] // TILE
         row = centers_ref[p, 0] % TILE
         col = centers_ref[p, 1] % TILE
         info = jnp.where(lane == 0, row, jnp.where(lane == 1, col, jnp.where(lane == 2, 1, 0)))
-        info_ref[owners[p]] = info.astype(jnp.float32).astype(jnp.bfloat16)
-    copies.append(
-        pltpu.make_async_copy(info_ref, sent_hbm.at[:, pl.ds(width, SLOT_PAD)], sems.at[count])
-    )
-    copies[-1].start()
-    for copy in copies:
-        copy.wait()
+        sent_ref[owner, :width] = pat_ref[p]
+        sent_ref[owner, width:] = info.astype(jnp.float32).astype(bf16)
 
 
 def parcels(centers, patterns, slots):
-    count, width, _ = patterns.shape
-    hbm = pl.BlockSpec(memory_space=pltpu.HBM)
+    width = patterns.shape[1]
+    vmem = pl.BlockSpec(memory_space=pltpu.VMEM)
     return pl.pallas_call(
         parcel_kernel,
         out_shape=jax.ShapeDtypeStruct((slots, width + SLOT_PAD, width), jnp.bfloat16),
-        in_specs=[pl.BlockSpec(memory_space=pltpu.SMEM), hbm],
-        out_specs=hbm,
-        scratch_shapes=[
-            pltpu.VMEM((slots, SLOT_PAD, width), jnp.bfloat16),
-            pltpu.SemaphoreType.DMA((count + 1,)),
-        ],
+        in_specs=[pl.BlockSpec(memory_space=pltpu.SMEM), vmem],
+        out_specs=vmem,
         compiler_params=pltpu.CompilerParams(vmem_limit_bytes=56 << 20),
     )(centers, patterns)
 

time: 106 us -> 98 us (0.925)
  Pallas kernels: 42 us -> 34.1 us
    pallas_call x1, Pallas kernels: 9.77 us -> 2.09 us  [parcels(): pl.pallas_call(parcel_kernel, out_shape=jax.ShapeDtypeStruct((slots, widt...]
  transfers between devices with their start and end apart: 9 -> 9, of which waited for: 7 -> 7; matrix products, arithmetic and copies ran while one was open for 1% -> 1% of each run, Pallas kernels for 9% -> 2%
where the time goes in v2:
time: 98 us; the launch traced here: 96.4 us
  Pallas kernels  34.1 us (35%)
  starting transfers between devices  29.2 us (30%)
  waiting for transfers between devices  28.1 us (29%)
  other arithmetic  4.44 us (5%)
    pallas_call x1, Pallas kernels, run_windows(): pl.pallas_call(functools.partial(windows_kernel, half), out_shape=(jax.Sh...  32.1 us
    ppermute x8, starting transfers between devices, shift(): return lax.ppermute(cells, axis, pairs)  22.6 us
    ppermute x8, waiting for transfers between devices, shift(): return lax.ppermute(cells, axis, pairs)  18.1 us
    all_to_all x1, waiting for transfers between devices, per_device(): got = lax.all_to_all(sent, 'tx', split_axis=0, concat_axis=0, tiled=True)  9.98 us
    all_to_all x1, starting transfers between devices, per_device(): got = lax.all_to_all(sent, 'tx', split_axis=0, concat_axis=0, tiled=True)  6.54 us
    pallas_call x1, Pallas kernels, parcels(): pl.pallas_call(parcel_kernel, out_shape=jax.ShapeDtypeStruct((slots, widt...  2.09 us
  transfers between devices with their start and end apart: 9, of which 7 were waited for; matrix products, arithmetic and copies ran while one was open for 1% of the time, Pallas kernels for 2%

profile of v2, /device:TPU:29, one launch (start us, length us, event | category | flops | bytes accessed | tf_op | source)
XLA Modules:
  0.0 96.4 jit_solution(15659929730849218005)
XLA Ops:
  0.0 1.3 %convert_element_type.33 = bf16[4,256,256]{2,1,0:T(8,128)(2,1)S(1)} convert(f32[4,256,256]{2,1,0:T(8,128)} %own_hbm.1) | non-fusion elementwise | flops 262144 | bytes 1572864 | tf_op jit(solution)/shard_map/convert_element_type | solution.py:324
  1.3 2.4 %collective-permute-start.1 = (bf16[4,128,256]{2,1,0:T(8,128)(2,1)S(1)}, bf16[4,128,256]{2,1,0:T(8,128)(2,1)S(1)}, u32[]{:S(2)}, u32[]{:S(2)}) collective-permute-start(bf16[4,128,256]{2,1,0:T(8,128)(2,1)S(1)} %get-tuple-element.19), channel_id=1, source_target_pairs={{8,0},{16,8},{24,16},{32,24},{40,32},{48,40},{56,48},{64,56},{72,6... | collective-permute-start | bytes 786440 | tf_op jit(solution)/shard_map/ppermute | solution.py:314
  3.7 5.0 %collective-permute-start = (bf16[4,128,256]{2,1,0:T(8,128)(2,1)S(1)}, bf16[4,128,256]{2,1,0:T(8,128)(2,1)S(1)}, u32[]{:S(2)}, u32[]{:S(2)}) collective-permute-start(bf16[4,128,256]{2,1,0:T(8,128)(2,1)S(1)} %get-tuple-element.20), channel_id=1, source_target_pairs={{0,8},{8,16},{16,24},{24,32},{32,40},{40,48},{48,56},{56,64},{64,7... | collective-permute-start | bytes 786440 | tf_op jit(solution)/shard_map/ppermute | solution.py:314
  8.7 2.1 %shard_map.55 = bf16[8,272,256]{2,1,0:T(8,128)(2,1)} custom-call(s32[2,2]{1,0:T(2,128)} %centers_ref.1, bf16[2,256,256]{2,1,0:T(8,128)(2,1)} %pat_ref.1), custom_call_target="tpu_custom_call" | custom-call | tf_op jit(solution)/shard_map/pallas_call | solution.py:302
  10.8 6.5 %all-to-all-start = ((bf16[8,272,256]{2,1,0:T(8,128)(2,1)}), bf16[8,272,256]{2,1,0:T(8,128)(2,1)S(1)}, u32[]{:S(2)}, u32[]{:S(2)}) async-start(bf16[8,272,256]{2,1,0:T(8,128)(2,1)} %shard_map.55), calls=%async_computation | async-start | bytes 2228224 | tf_op jit(solution)/shard_map/all_to_all | solution.py:329
  17.4 0.1 fusion.3
  17.5 0.0 collective-permute-done.1.down_hbm
  17.5 0.0 copy-start.2
  17.5 0.0 collective-permute-done.up_hbm
  17.6 0.0 copy-start.3
  17.7 3.5 %collective-permute-start.2 = (bf16[4,512,128]{2,1,0:T(8,128)(2,1)S(1)}, bf16[4,512,128]{2,1,0:T(8,128)(2,1)S(1)}, u32[]{:S(2)}, u32[]{:S(2)}) collective-permute-start(bf16[4,512,128]{2,1,0:T(8,128)(2,1)S(1)} %pad_maximum_fusion), channel_id=1, source_target_pairs={{0,1},{1,2},{2,3},{3,4},{4,5},{5,6},{6,7},{8,9},{9,10},{10,11},{11... | collective-permute-start | bytes 1572872 | tf_op jit(solution)/shard_map/ppermute | solution.py:314
  21.3 1.9 %collective-permute-start.3 = (bf16[4,512,128]{2,1,0:T(8,128)(2,1)S(1)}, bf16[4,512,128]{2,1,0:T(8,128)(2,1)}, u32[]{:S(2)}, u32[]{:S(2)}) collective-permute-start(bf16[4,512,128]{2,1,0:T(8,128)(2,1)S(1)} %pad_maximum_fusion.1), channel_id=1, source_target_pairs={{1,0},{2,1},{3,2},{4,3},{5,4},{6,5},{7,6},{9,8},{10,9},{11,10},{12... | collective-permute-start | bytes 1572872 | tf_op jit(solution)/shard_map/ppermute | solution.py:314
  23.2 10.0 %all-to-all-done.pat_hbm = bf16[8,272,256]{2,1,0:T(8,128)(2,1)S(1)} async-done(((bf16[8,272,256]{2,1,0:T(8,128)(2,1)}), bf16[8,272,256]{2,1,0:T(8,128)(2,1)S(1)}, u32[]{:S(2)}, u32[]{:S(2)}) %all-to-all-start) | async-done | bytes 1114144 | tf_op jit(solution)/shard_map/all_to_all | solution.py:329
  33.2 0.0 copy-start
  33.2 0.6 fusion
  33.8 1.9 %collective-permute-done.2.west_hbm = bf16[4,512,128]{2,1,0:T(8,128)(2,1)S(1)} collective-permute-done((bf16[4,512,128]{2,1,0:T(8,128)(2,1)S(1)}, bf16[4,512,128]{2,1,0:T(8,128)(2,1)S(1)}, u32[]{:S(2)}, u32[]{:S(2)}) %collective-permute-start.2) | collective-permute-done | bytes 524320 | tf_op jit(solution)/shard_map/ppermute | solution.py:314
  35.7 0.0 copy-start.4
  35.7 1.9 %collective-permute-done.3.east_hbm = bf16[4,512,128]{2,1,0:T(8,128)(2,1)} collective-permute-done((bf16[4,512,128]{2,1,0:T(8,128)(2,1)S(1)}, bf16[4,512,128]{2,1,0:T(8,128)(2,1)}, u32[]{:S(2)}, u32[]{:S(2)}) %collective-permute-start.3) | collective-permute-done | bytes 524320 | tf_op jit(solution)/shard_map/ppermute | solution.py:314
  37.6 0.0 copy-done.2
  37.6 0.0 copy-done.3
  37.6 0.0 copy-done
  37.6 0.0 copy-done.4
  37.6 32.1 %shard_map.56 = (f32[4,512,256]{2,1,0:T(8,128)}, bf16[4,512,128]{2,1,0:T(8,128)(2,1)}, bf16[4,512,128]{2,1,0:T(8,128)(2,1)}) custom-call(s32[8,3]{1,0:T(8,128)} %bitcast.1, f32[4,256,256]{2,1,0:T(8,128)} %own_hbm.1, bf16[4,128,256]{2,1,0:T(8,128)(2,1)} %copy-done.3, bf16[4,128,256]{2,1,0:T(8,128)(2,1)} %copy-done.2, bf16[4,512,128]{2,1,0:T(8,128)(2,1)} %copy-done.4, ...), custom_call_target="tpu_custom_call" | custom-call | tf_op jit(solution)/shard_map/pallas_call | solution.py:248
  69.7 1.9 %collective-permute-start.4 = (bf16[4,512,128]{2,1,0:T(8,128)(2,1)}, bf16[4,512,128]{2,1,0:T(8,128)(2,1)S(1)}, u32[]{:S(2)}, u32[]{:S(2)}) collective-permute-start(bf16[4,512,128]{2,1,0:T(8,128)(2,1)} %get-tuple-element.9), channel_id=1, source_target_pairs={{0,1},{1,2},{2,3},{3,4},{4,5},{5,6},{6,7},{8,9},{9,10},{10,11},{11... | collective-permute-start | bytes 1572872 | tf_op jit(solution)/shard_map/ppermute | solution.py:314
  71.6 0.0 copy-start.1
  71.6 2.6 %collective-permute-start.5 = (bf16[4,512,128]{2,1,0:T(8,128)(2,1)}, bf16[4,512,128]{2,1,0:T(8,128)(2,1)S(1)}, u32[]{:S(2)}, u32[]{:S(2)}) collective-permute-start(bf16[4,512,128]{2,1,0:T(8,128)(2,1)} %get-tuple-element.10), channel_id=1, source_target_pairs={{1,0},{2,1},{3,2},{4,3},{5,4},{6,5},{7,6},{9,8},{10,9},{11,10},{12... | collective-permute-start | bytes 1572872 | tf_op jit(solution)/shard_map/ppermute | solution.py:314
  74.2 3.8 %collective-permute-done.4 = bf16[4,512,128]{2,1,0:T(8,128)(2,1)S(1)} collective-permute-done((bf16[4,512,128]{2,1,0:T(8,128)(2,1)}, bf16[4,512,128]{2,1,0:T(8,128)(2,1)S(1)}, u32[]{:S(2)}, u32[]{:S(2)}) %collective-permute-start.4) | collective-permute-done | bytes 524320 | tf_op jit(solution)/shard_map/ppermute | solution.py:314
  78.0 4.7 %collective-permute-done.5 = bf16[4,512,128]{2,1,0:T(8,128)(2,1)S(1)} collective-permute-done((bf16[4,512,128]{2,1,0:T(8,128)(2,1)}, bf16[4,512,128]{2,1,0:T(8,128)(2,1)S(1)}, u32[]{:S(2)}, u32[]{:S(2)}) %collective-permute-start.5) | collective-permute-done | bytes 524320 | tf_op jit(solution)/shard_map/ppermute | solution.py:314
  82.8 1.3 %add_convert_fusion.1 = (bf16[4,128,256]{2,1,0:T(8,128)(2,1)S(1)}, bf16[4,128,256]{2,1,0:T(8,128)(2,1)S(1)}) fusion(f32[4,512,256]{2,1,0:T(8,128)} %get-tuple-element.8, bf16[4,128,128]{2,1,0:T(8,128)(2,1)S(1)} %get-tuple-element.15, bf16[4,128,128]{2,1,0:T(8,128)(2,1)S(1)} %get-tuple-element.13, bf16[4,128,128]{2,1,0:T(8,128)(2,1)S(1)} %get-tuple-element.16, ...), kind=kLoop, calls=%fused_computation.4 | loop fusion | flops 1572864 | bytes 2097152 | tf_op jit(solution)/shard_map/convert_element_type | solution.py:349
  84.1 1.9 %collective-permute-start.6 = (bf16[4,128,256]{2,1,0:T(8,128)(2,1)S(1)}, bf16[4,128,256]{2,1,0:T(8,128)(2,1)S(1)}, u32[]{:S(2)}, u32[]{:S(2)}) collective-permute-start(bf16[4,128,256]{2,1,0:T(8,128)(2,1)S(1)} %get-tuple-element.11), channel_id=1, source_target_pairs={{0,8},{8,16},{16,24},{24,32},{32,40},{40,48},{48,56},{56,64},{64,7... | collective-permute-start | bytes 786440 | tf_op jit(solution)/shard_map/ppermute | solution.py:314
  86.0 3.4 %collective-permute-start.7 = (bf16[4,128,256]{2,1,0:T(8,128)(2,1)S(1)}, bf16[4,128,256]{2,1,0:T(8,128)(2,1)S(1)}, u32[]{:S(2)}, u32[]{:S(2)}) collective-permute-start(bf16[4,128,256]{2,1,0:T(8,128)(2,1)S(1)} %get-tuple-element.12), channel_id=1, source_target_pairs={{8,0},{16,8},{24,16},{32,24},{40,32},{48,40},{56,48},{64,56},{72,6... | collective-permute-start | bytes 786440 | tf_op jit(solution)/shard_map/ppermute | solution.py:314
  89.4 1.8 %collective-permute-done.6 = bf16[4,128,256]{2,1,0:T(8,128)(2,1)S(1)} collective-permute-done((bf16[4,128,256]{2,1,0:T(8,128)(2,1)S(1)}, bf16[4,128,256]{2,1,0:T(8,128)(2,1)S(1)}, u32[]{:S(2)}, u32[]{:S(2)}) %collective-permute-start.6) | collective-permute-done | bytes 262176 | tf_op jit(solution)/shard_map/ppermute | solution.py:314
  91.2 4.0 %collective-permute-done.7 = bf16[4,128,256]{2,1,0:T(8,128)(2,1)S(1)} collective-permute-done((bf16[4,128,256]{2,1,0:T(8,128)(2,1)S(1)}, bf16[4,128,256]{2,1,0:T(8,128)(2,1)S(1)}, u32[]{:S(2)}, u32[]{:S(2)}) %collective-permute-start.7) | collective-permute-done | bytes 262176 | tf_op jit(solution)/shard_map/ppermute | solution.py:314
  95.2 0.0 copy-done.1
  95.3 1.1 %convert_add_fusion = f32[4,256,256]{2,1,0:T(8,128)} fusion(f32[4,512,256]{2,1,0:T(8,128)S(1)} %copy-done.1, bf16[4,256,128]{2,1,0:T(8,128)(2,1)S(1)} %slice.82, bf16[4,256,128]{2,1,0:T(8,128)(2,1)S(1)} %slice.81, bf16[4,128,256]{2,1,0:T(8,128)(2,1)S(1)} %collective-permute-done.7, bf16[4,128,256]{2,1,0:T(8,128)(2,1)S(1)} %collective-permute-done.6), kind=kLoop, calls=%fused_computation | loop fusion | flops 2621440 | bytes 3145728 | tf_op jit(solution)/shard_map/add | solution.py:351
  (9 shorter events, 0.3 us)
Async XLA Ops:
  1.3 16.1 %collective-permute-start.1 = (bf16[4,128,256]{2,1,0:T(8,128)(2,1)S(1)}, bf16[4,128,256]{2,1,0:T(8,128)(2,1)S(1)}, u32[]{:S(2)}, u32[]{:S(2)}) collective-permute-start(bf16[4,128,256]{2,1,0:T(8,128)(2,1)S(1)} %get-tuple-element.19), channel_id=1, source_target_pairs={{8,0},{16,8},{24,16},{32,24},{40,32},{48,40},{56,48},{64,56},{72,6... | collective-permute-start | bytes 786440 | tf_op jit(solution)/shard_map/ppermute | solution.py:314
  3.7 13.8 %collective-permute-start = (bf16[4,128,256]{2,1,0:T(8,128)(2,1)S(1)}, bf16[4,128,256]{2,1,0:T(8,128)(2,1)S(1)}, u32[]{:S(2)}, u32[]{:S(2)}) collective-permute-start(bf16[4,128,256]{2,1,0:T(8,128)(2,1)S(1)} %get-tuple-element.20), channel_id=1, source_target_pairs={{0,8},{8,16},{16,24},{24,32},{32,40},{40,48},{48,56},{56,64},{64,7... | collective-permute-start | bytes 786440 | tf_op jit(solution)/shard_map/ppermute | solution.py:314
  10.8 22.3 %all-to-all-start = ((bf16[8,272,256]{2,1,0:T(8,128)(2,1)}), bf16[8,272,256]{2,1,0:T(8,128)(2,1)S(1)}, u32[]{:S(2)}, u32[]{:S(2)}) async-start(bf16[8,272,256]{2,1,0:T(8,128)(2,1)} %shard_map.55), calls=%async_computation | async-start | bytes 2228224 | tf_op jit(solution)/shard_map/all_to_all | solution.py:329
  17.5 20.1 %copy-start.2 = (bf16[4,128,256]{2,1,0:T(8,128)(2,1)}, bf16[4,128,256]{2,1,0:T(8,128)(2,1)S(1)}, u32[]{:S(2)}) copy-start(bf16[4,128,256]{2,1,0:T(8,128)(2,1)S(1)} %collective-permute-done.1.down_hbm) | copy-start | bytes 786436
  17.6 20.0 %copy-start.3 = (bf16[4,128,256]{2,1,0:T(8,128)(2,1)}, bf16[4,128,256]{2,1,0:T(8,128)(2,1)S(1)}, u32[]{:S(2)}) copy-start(bf16[4,128,256]{2,1,0:T(8,128)(2,1)S(1)} %collective-permute-done.up_hbm) | copy-start | bytes 786436
  17.7 18.0 %collective-permute-start.2 = (bf16[4,512,128]{2,1,0:T(8,128)(2,1)S(1)}, bf16[4,512,128]{2,1,0:T(8,128)(2,1)S(1)}, u32[]{:S(2)}, u32[]{:S(2)}) collective-permute-start(bf16[4,512,128]{2,1,0:T(8,128)(2,1)S(1)} %pad_maximum_fusion), channel_id=1, source_target_pairs={{0,1},{1,2},{2,3},{3,4},{4,5},{5,6},{6,7},{8,9},{9,10},{10,11},{11... | collective-permute-start | bytes 1572872 | tf_op jit(solution)/shard_map/ppermute | solution.py:314
  21.3 16.3 %collective-permute-start.3 = (bf16[4,512,128]{2,1,0:T(8,128)(2,1)S(1)}, bf16[4,512,128]{2,1,0:T(8,128)(2,1)}, u32[]{:S(2)}, u32[]{:S(2)}) collective-permute-start(bf16[4,512,128]{2,1,0:T(8,128)(2,1)S(1)} %pad_maximum_fusion.1), channel_id=1, source_target_pairs={{1,0},{2,1},{3,2},{4,3},{5,4},{6,5},{7,6},{9,8},{10,9},{11,10},{12... | collective-permute-start | bytes 1572872 | tf_op jit(solution)/shard_map/ppermute | solution.py:314
  33.2 4.4 %copy-start = (bf16[8,272,256]{2,1,0:T(8,128)(2,1)}, bf16[8,272,256]{2,1,0:T(8,128)(2,1)S(1)}, u32[]{:S(2)}) copy-start(bf16[8,272,256]{2,1,0:T(8,128)(2,1)S(1)} %all-to-all-done.pat_hbm) | copy-start | bytes 3342340
  35.7 1.9 %copy-start.4 = (bf16[4,512,128]{2,1,0:T(8,128)(2,1)}, bf16[4,512,128]{2,1,0:T(8,128)(2,1)S(1)}, u32[]{:S(2)}) copy-start(bf16[4,512,128]{2,1,0:T(8,128)(2,1)S(1)} %collective-permute-done.2.west_hbm) | copy-start | bytes 1572868
  69.7 8.3 %collective-permute-start.4 = (bf16[4,512,128]{2,1,0:T(8,128)(2,1)}, bf16[4,512,128]{2,1,0:T(8,128)(2,1)S(1)}, u32[]{:S(2)}, u32[]{:S(2)}) collective-permute-start(bf16[4,512,128]{2,1,0:T(8,128)(2,1)} %get-tuple-element.9), channel_id=1, source_target_pairs={{0,1},{1,2},{2,3},{3,4},{4,5},{5,6},{6,7},{8,9},{9,10},{10,11},{11... | collective-permute-start | bytes 1572872 | tf_op jit(solution)/shard_map/ppermute | solution.py:314
  71.6 23.7 %copy-start.1 = (f32[4,512,256]{2,1,0:T(8,128)S(1)}, f32[4,512,256]{2,1,0:T(8,128)}, u32[]{:S(2)}) copy-start(f32[4,512,256]{2,1,0:T(8,128)} %get-tuple-element.8) | copy-start | bytes 6291460
  71.6 11.1 %collective-permute-start.5 = (bf16[4,512,128]{2,1,0:T(8,128)(2,1)}, bf16[4,512,128]{2,1,0:T(8,128)(2,1)S(1)}, u32[]{:S(2)}, u32[]{:S(2)}) collective-permute-start(bf16[4,512,128]{2,1,0:T(8,128)(2,1)} %get-tuple-element.10), channel_id=1, source_target_pairs={{1,0},{2,1},{3,2},{4,3},{5,4},{6,5},{7,6},{9,8},{10,9},{11,10},{12... | collective-permute-start | bytes 1572872 | tf_op jit(solution)/shard_map/ppermute | solution.py:314
  84.1 7.1 %collective-permute-start.6 = (bf16[4,128,256]{2,1,0:T(8,128)(2,1)S(1)}, bf16[4,128,256]{2,1,0:T(8,128)(2,1)S(1)}, u32[]{:S(2)}, u32[]{:S(2)}) collective-permute-start(bf16[4,128,256]{2,1,0:T(8,128)(2,1)S(1)} %get-tuple-element.11), channel_id=1, source_target_pairs={{0,8},{8,16},{16,24},{24,32},{32,40},{40,48},{48,56},{56,64},{64,7... | collective-permute-start | bytes 786440 | tf_op jit(solution)/shard_map/ppermute | solution.py:314
  86.0 9.2 %collective-permute-start.7 = (bf16[4,128,256]{2,1,0:T(8,128)(2,1)S(1)}, bf16[4,128,256]{2,1,0:T(8,128)(2,1)S(1)}, u32[]{:S(2)}, u32[]{:S(2)}) collective-permute-start(bf16[4,128,256]{2,1,0:T(8,128)(2,1)S(1)} %get-tuple-element.12), channel_id=1, source_target_pairs={{8,0},{16,8},{24,16},{32,24},{40,32},{48,40},{56,48},{64,56},{72,6... | collective-permute-start | bytes 786440 | tf_op jit(solution)/shard_map/ppermute | solution.py:314

commit v3 on v2

--- a/solution.py
+++ b/solution.py
@@ -15,6 +15,8 @@
 TILE = 256
 LANES = 128
 PITCH = 5
+GROUP = 2
+STREAMS = 2
 
 
 def sin_cos_coefs(limit):
@@ -23,8 +25,8 @@
     v = np.sqrt(u) * limit
     t = 0.25 * v
     scale = limit * limit
-    a = np.polynomial.polynomial.polyfit(u, 2 * np.sin(t) / v, 5) / scale ** np.arange(6)
-    b = np.polynomial.polynomial.polyfit(u, np.cos(t), 5) / scale ** np.arange(6)
+    a = np.polynomial.polynomial.polyfit(u, 2 * np.sin(t) / v, 4) / scale ** np.arange(5)
+    b = np.polynomial.polynomial.polyfit(u, np.cos(t), 4) / scale ** np.arange(5)
     return [float(np.float32(x)) for x in a], [float(np.float32(x)) for x in b]
 
 
@@ -117,34 +119,40 @@
     def chunks():
         return [slice(k * rows, (k + 1) * rows) for k in range(width // rows)]
 
-    def one_window(slot, cs_ref, phi_ref, s_ref, t_ref):
-        row = where_ref[slot, 0]
-        col = where_ref[slot, 1]
-        block = col // LANES
-        turn = col - block * LANES
-        back = jnp.where(turn == 0, 0, LANES - turn)
+    def group(slot_list, cs_ref, phi_ref, s_ref, t_ref):
+        places = []
         lane = lax.broadcasted_iota(jnp.int32, (rows, LANES), 1)
-        low = lane < LANES - turn
-        high = lane >= turn
-
-        def modulate(s, k, re, im):
+        for slot in slot_list:
+            row = where_ref[slot, 0]
+            col = where_ref[slot, 1]
+            block = col // LANES
+            turn = col - block * LANES
+            back = jnp.where(turn == 0, 0, LANES - turn)
+            weight = jnp.where(where_ref[slot, 2] > 0, 1.0, 0.0)
+            places.append((row, block, turn, back, lane < LANES - turn, lane >= turn, weight))
+
+        def modulate(w, s, k, re, im):
+            row, block, turn, back, low, high, weight = places[w]
             parts = [
                 pltpu.roll(ext_ref[s, every(row + k.start, rows, block + j)], back, 1)
                 for j in range(halves + 1)
             ]
             for j in range(halves):
                 c = slice(j * LANES, (j + 1) * LANES)
+                into = slice(w * width + c.start, w * width + c.stop)
                 sin, cos = sin_cos_half(jnp.where(low, parts[j], parts[j + 1]))
-                cs_ref[s, 0, k, c] = cos
-                cs_ref[s, 1, k, c] = sin
                 new_re = re[:, c] * cos - im[:, c] * sin
                 new_im = re[:, c] * sin + im[:, c] * cos
-                phi_ref[s, 0, k, c] = new_re
-                phi_ref[s, 1, k, c] = new_im
-                s_ref[k, c] = new_re.astype(bf16)
-                s_ref[width + k.start : width + k.stop, c] = new_im.astype(bf16)
-
-        def deposit(s, k, grad):
+                if s:
+                    cs_ref[w, s, 0, k, c] = cos
+                    cs_ref[w, s, 1, k, c] = sin
+                phi_ref[w, s, 0, k, c] = new_re
+                phi_ref[w, s, 1, k, c] = new_im
+                s_ref[k, into] = new_re.astype(bf16)
+                s_ref[width + k.start : width + k.stop, into] = new_im.astype(bf16)
+
+        def deposit(w, s, k, grad):
+            row, block, turn, back, low, high, weight = places[w]
             parts = [pltpu.roll(grad[:, j * LANES : (j + 1) * LANES], turn, 1) for j in range(halves)]
             zero = jnp.zeros((rows, LANES), f32)
             for j in range(halves + 1):
@@ -152,70 +160,91 @@
                 before = parts[j - 1] if j else zero
                 acc_ref[s, every(row + k.start, rows, block + j)] += jnp.where(high, here, before)
 
-        def apply(table):
-            mid = dot(tab_ref[table], s_ref[...]).astype(bf16)
-            t_ref[:, :width] = mid[:width]
-            t_ref[:, width:] = mid[width:]
-            return dot(t_ref[...], tab_ref[table + 1])
-
-        def apply_back(table):
-            mid = dot(t_ref[...], tab_ref[table]).astype(bf16)
-            s_ref[:width] = mid[:, :width]
-            s_ref[width:] = mid[:, width:]
-            return dot(tab_ref[table + 1], s_ref[...])
-
-        for k in chunks():
-            modulate(0, k, probe_ref[0, k], probe_ref[1, k])
-        for s in range(1, slices):
+        def span(w):
+            return slice(w * width, (w + 1) * width)
+
+        def left(table):
+            return dot(tab_ref[table], s_ref[...])
+
+        def right(table):
+            return dot(t_ref[...], tab_ref[table])
+
+        many = range(len(slot_list))
+        for w in many:
+            for k in chunks():
+                modulate(w, 0, k, probe_ref[0, k], probe_ref[1, k])
+        for s in range(1, slices + 1):
+            table = 2 if s == slices else 0
             yield
-            z = apply(0)
+            mid = left(table).astype(bf16)
+            for w in many:
+                t_ref[span(w), :width] = mid[:width, span(w)]
+                t_ref[span(w), width:] = mid[width:, span(w)]
+            z = right(table + 1)
             yield
-            for k in chunks():
-                modulate(s, k, z[k, :width], z[k, width:])
-        yield
-        z = apply(2)
-        yield
-        for k in chunks():
-            re, im = z[k, :width], z[k, width:]
-            excess = re * re + im * im - pat_ref[slot, k].astype(f32)
-            t_ref[k, :width] = (excess * re).astype(bf16)
-            t_ref[k, width:] = (excess * im).astype(bf16)
+            for w in many:
+                for k in chunks():
+                    own = slice(w * width + k.start, w * width + k.stop)
+                    re, im = z[own, :width], z[own, width:]
+                    if s < slices:
+                        modulate(w, s, k, re, im)
+                    else:
+                        excess = re * re + im * im - pat_ref[slot_list[w], k].astype(f32)
+                        t_ref[own, :width] = (excess * re).astype(bf16)
+                        t_ref[own, width:] = (excess * im).astype(bf16)
         for s in range(slices - 1, -1, -1):
+            table = 2 if s == slices - 1 else 0
             yield
-            g = apply_back(2 if s == slices - 1 else 0)
+            mid = right(table).astype(bf16)
+            for w in many:
+                s_ref[:width, span(w)] = mid[span(w), :width]
+                s_ref[width:, span(w)] = mid[span(w), width:]
+            g = left(table + 1)
             yield
-            for k in chunks():
-                re, im = g[k], g[width + k.start : width + k.stop]
-                grad = im * phi_ref[s, 0, k] - re * phi_ref[s, 1, k]
-                deposit(s, k, grad)
-                if s:
-                    cos, sin = cs_ref[s, 0, k], cs_ref[s, 1, k]
-                    t_ref[k, :width] = (re * cos + im * sin).astype(bf16)
-                    t_ref[k, width:] = (im * cos - re * sin).astype(bf16)
-
-    def list_slot(slot, filled):
-        order_ref[filled] = slot
-        return filled + where_ref[slot, 2]
-
-    filled = lax.fori_loop(0, slots, list_slot, 0)
-
-    def pair(number, carry):
-        first = one_window(order_ref[2 * number], *streams[:4])
-        second = one_window(order_ref[2 * number + 1], *streams[4:])
-        next(first)
+            for w in many:
+                for k in chunks():
+                    own = slice(w * width + k.start, w * width + k.stop)
+                    re, im = g[k, span(w)], g[width + k.start : width + k.stop, span(w)]
+                    grad = places[w][-1] * (im * phi_ref[w, s, 0, k] - re * phi_ref[w, s, 1, k])
+                    deposit(w, s, k, grad)
+                    if s:
+                        cos, sin = cs_ref[w, s, 0, k], cs_ref[w, s, 1, k]
+                        t_ref[own, :width] = (re * cos + im * sin).astype(bf16)
+                        t_ref[own, width:] = (im * cos - re * sin).astype(bf16)
+
+    def list_slots(wanted):
+        def body(slot, count):
+            filled = where_ref[slot, 2] > 0
+
+            @pl.when(filled == wanted)
+            def _():
+                order_ref[count] = slot
+
+            return count + jnp.where(filled == wanted, 1, 0)
+
+        return body
+
+    filled = lax.fori_loop(0, slots, list_slots(True), 0)
+    lax.fori_loop(0, slots, list_slots(False), filled)
+    batch = STREAMS * GROUP
+
+    def many_windows(number, carry):
+        running = []
+        for i in range(STREAMS):
+            base = number * batch + i * GROUP
+            chosen = [order_ref[base + w] for w in range(GROUP)]
+            running.append(group(chosen, *streams[4 * i : 4 * i + 4]))
+        for i, stream in enumerate(running):
+            for _ in range(STREAMS - 1 - i):
+                next(stream)
         alive = True
         while alive:
             alive = False
-            for stream in (first, second):
+            for stream in running:
                 alive = next(stream, True) is None or alive
         return carry
 
-    lax.fori_loop(0, filled // 2, pair, 0)
-
-    @pl.when(filled % 2 == 1)
-    def _():
-        for _ in one_window(order_ref[filled - 1], *streams[:4]):
-            pass
+    lax.fori_loop(0, (filled + batch - 1) // batch, many_windows, 0)
 
     stores = []
     for s in range(slices):
@@ -257,7 +286,7 @@
         scratch_shapes=[
             pltpu.VMEM((slices, tall * PITCH, LANES), f32),
             pltpu.VMEM((slices, tall * PITCH, LANES), f32),
-            pltpu.SMEM((patterns.shape[0] + 1,), jnp.int32),
+            pltpu.SMEM((patterns.shape[0],), jnp.int32),
         ]
         + [
             pltpu.VMEM(x.shape, x.dtype)
@@ -271,12 +300,12 @@
             pltpu.SemaphoreType.DMA((slices, 3)),
         ]
         + [
-            pltpu.VMEM((slices, 2, width, width), f32),
-            pltpu.VMEM((slices, 2, width, width), f32),
-            pltpu.VMEM((2 * width, width), bf16),
-            pltpu.VMEM((width, 2 * width), bf16),
+            pltpu.VMEM((GROUP, slices, 2, width, width), f32),
+            pltpu.VMEM((GROUP, slices, 2, width, width), f32),
+            pltpu.VMEM((2 * width, GROUP * width), bf16),
+            pltpu.VMEM((GROUP * width, 2 * width), bf16),
         ]
-        * 2,
+        * STREAMS,
         compiler_params=pltpu.CompilerParams(vmem_limit_bytes=56 << 20),
         interpret=interpret,
     )(where, own, up, down, west, east, probe, patterns, tables)

time: 98 us -> 97.1 us (level)
  Pallas kernels: 34.1 us -> 7.56 us
  starting transfers between devices: 29.2 us -> 54.4 us
    pallas_call x1, Pallas kernels: 32.1 us -> 5.47 us  [run_windows(): pl.pallas_call(functools.partial(windows_kernel, half), out_shape=(jax.Sh...]
    ppermute x8, starting transfers between devices: 22.6 us -> 47.8 us  [shift(): return lax.ppermute(cells, axis, pairs)]
where the time goes in v3:
time: 97.1 us; the launch traced here: 95.5 us
  starting transfers between devices  54.4 us (56%)
  waiting for transfers between devices  28.6 us (29%)
  Pallas kernels  7.56 us (8%)
  other arithmetic  4.44 us (5%)
    ppermute x8, starting transfers between devices, shift(): return lax.ppermute(cells, axis, pairs)  47.8 us
    ppermute x8, waiting for transfers between devices, shift(): return lax.ppermute(cells, axis, pairs)  18.6 us
    all_to_all x1, waiting for transfers between devices, per_device(): got = lax.all_to_all(sent, 'tx', split_axis=0, concat_axis=0, tiled=True)  9.98 us
    all_to_all x1, starting transfers between devices, per_device(): got = lax.all_to_all(sent, 'tx', split_axis=0, concat_axis=0, tiled=True)  6.54 us
    pallas_call x1, Pallas kernels, run_windows(): pl.pallas_call(functools.partial(windows_kernel, half), out_shape=(jax.Sh...  5.47 us
    pallas_call x1, Pallas kernels, parcels(): pl.pallas_call(parcel_kernel, out_shape=jax.ShapeDtypeStruct((slots, widt...  2.09 us
  transfers between devices with their start and end apart: 9, of which 7 were waited for; matrix products, arithmetic and copies ran while one was open for 1% of the time, Pallas kernels for 2%

profile of v3, /device:TPU:29, one launch (start us, length us, event | category | flops | bytes accessed | tf_op | source)
XLA Modules:
  0.0 95.5 jit_solution(3963371431150156438)
XLA Ops:
  0.0 1.3 %convert_element_type.33 = bf16[4,256,256]{2,1,0:T(8,128)(2,1)S(1)} convert(f32[4,256,256]{2,1,0:T(8,128)} %own_hbm.1) | non-fusion elementwise | flops 262144 | bytes 1572864 | tf_op jit(solution)/shard_map/convert_element_type | solution.py:353
  1.3 2.4 %collective-permute-start.1 = (bf16[4,128,256]{2,1,0:T(8,128)(2,1)S(1)}, bf16[4,128,256]{2,1,0:T(8,128)(2,1)S(1)}, u32[]{:S(2)}, u32[]{:S(2)}) collective-permute-start(bf16[4,128,256]{2,1,0:T(8,128)(2,1)S(1)} %get-tuple-element.19), channel_id=1, source_target_pairs={{8,0},{16,8},{24,16},{32,24},{40,32},{48,40},{56,48},{64,56},{72,6... | collective-permute-start | bytes 786440 | tf_op jit(solution)/shard_map/ppermute | solution.py:343
  3.7 5.0 %collective-permute-start = (bf16[4,128,256]{2,1,0:T(8,128)(2,1)S(1)}, bf16[4,128,256]{2,1,0:T(8,128)(2,1)S(1)}, u32[]{:S(2)}, u32[]{:S(2)}) collective-permute-start(bf16[4,128,256]{2,1,0:T(8,128)(2,1)S(1)} %get-tuple-element.20), channel_id=1, source_target_pairs={{0,8},{8,16},{16,24},{24,32},{32,40},{40,48},{48,56},{56,64},{64,7... | collective-permute-start | bytes 786440 | tf_op jit(solution)/shard_map/ppermute | solution.py:343
  8.7 2.1 %shard_map.55 = bf16[8,272,256]{2,1,0:T(8,128)(2,1)} custom-call(s32[2,2]{1,0:T(2,128)} %centers_ref.1, bf16[2,256,256]{2,1,0:T(8,128)(2,1)} %pat_ref.1), custom_call_target="tpu_custom_call" | custom-call | tf_op jit(solution)/shard_map/pallas_call | solution.py:331
  10.8 6.5 %all-to-all-start = ((bf16[8,272,256]{2,1,0:T(8,128)(2,1)}), bf16[8,272,256]{2,1,0:T(8,128)(2,1)S(1)}, u32[]{:S(2)}, u32[]{:S(2)}) async-start(bf16[8,272,256]{2,1,0:T(8,128)(2,1)} %shard_map.55), calls=%async_computation | async-start | bytes 2228224 | tf_op jit(solution)/shard_map/all_to_all | solution.py:358
  17.4 0.1 fusion.3
  17.5 0.0 collective-permute-done.1.down_hbm
  17.5 0.0 copy-start.2
  17.5 0.0 collective-permute-done.up_hbm
  17.6 0.0 copy-start.3
  17.7 3.5 %collective-permute-start.2 = (bf16[4,512,128]{2,1,0:T(8,128)(2,1)S(1)}, bf16[4,512,128]{2,1,0:T(8,128)(2,1)S(1)}, u32[]{:S(2)}, u32[]{:S(2)}) collective-permute-start(bf16[4,512,128]{2,1,0:T(8,128)(2,1)S(1)} %pad_maximum_fusion), channel_id=1, source_target_pairs={{0,1},{1,2},{2,3},{3,4},{4,5},{5,6},{6,7},{8,9},{9,10},{10,11},{11... | collective-permute-start | bytes 1572872 | tf_op jit(solution)/shard_map/ppermute | solution.py:343
  21.3 1.9 %collective-permute-start.3 = (bf16[4,512,128]{2,1,0:T(8,128)(2,1)S(1)}, bf16[4,512,128]{2,1,0:T(8,128)(2,1)}, u32[]{:S(2)}, u32[]{:S(2)}) collective-permute-start(bf16[4,512,128]{2,1,0:T(8,128)(2,1)S(1)} %pad_maximum_fusion.1), channel_id=1, source_target_pairs={{1,0},{2,1},{3,2},{4,3},{5,4},{6,5},{7,6},{9,8},{10,9},{11,10},{12... | collective-permute-start | bytes 1572872 | tf_op jit(solution)/shard_map/ppermute | solution.py:343
  23.2 10.0 %all-to-all-done.pat_hbm = bf16[8,272,256]{2,1,0:T(8,128)(2,1)S(1)} async-done(((bf16[8,272,256]{2,1,0:T(8,128)(2,1)}), bf16[8,272,256]{2,1,0:T(8,128)(2,1)S(1)}, u32[]{:S(2)}, u32[]{:S(2)}) %all-to-all-start) | async-done | bytes 1114144 | tf_op jit(solution)/shard_map/all_to_all | solution.py:358
  33.2 0.0 copy-start
  33.2 0.6 fusion
  33.8 1.9 %collective-permute-done.2.west_hbm = bf16[4,512,128]{2,1,0:T(8,128)(2,1)S(1)} collective-permute-done((bf16[4,512,128]{2,1,0:T(8,128)(2,1)S(1)}, bf16[4,512,128]{2,1,0:T(8,128)(2,1)S(1)}, u32[]{:S(2)}, u32[]{:S(2)}) %collective-permute-start.2) | collective-permute-done | bytes 524320 | tf_op jit(solution)/shard_map/ppermute | solution.py:343
  35.7 0.0 copy-start.4
  35.7 1.9 %collective-permute-done.3.east_hbm = bf16[4,512,128]{2,1,0:T(8,128)(2,1)} collective-permute-done((bf16[4,512,128]{2,1,0:T(8,128)(2,1)S(1)}, bf16[4,512,128]{2,1,0:T(8,128)(2,1)}, u32[]{:S(2)}, u32[]{:S(2)}) %collective-permute-start.3) | collective-permute-done | bytes 524320 | tf_op jit(solution)/shard_map/ppermute | solution.py:343
  37.6 0.0 copy-done.2
  37.6 0.0 copy-done.3
  37.6 0.0 copy-done
  37.6 0.0 copy-done.4
  37.6 5.5 %shard_map.56 = (f32[4,512,256]{2,1,0:T(8,128)}, bf16[4,512,128]{2,1,0:T(8,128)(2,1)}, bf16[4,512,128]{2,1,0:T(8,128)(2,1)}) custom-call(s32[8,3]{1,0:T(8,128)} %bitcast.1, f32[4,256,256]{2,1,0:T(8,128)} %own_hbm.1, bf16[4,128,256]{2,1,0:T(8,128)(2,1)} %copy-done.3, bf16[4,128,256]{2,1,0:T(8,128)(2,1)} %copy-done.2, bf16[4,512,128]{2,1,0:T(8,128)(2,1)} %copy-done.4, ...), custom_call_target="tpu_custom_call" | custom-call | tf_op jit(solution)/shard_map/pallas_call | solution.py:277
  43.1 27.6 %collective-permute-start.4 = (bf16[4,512,128]{2,1,0:T(8,128)(2,1)}, bf16[4,512,128]{2,1,0:T(8,128)(2,1)S(1)}, u32[]{:S(2)}, u32[]{:S(2)}) collective-permute-start(bf16[4,512,128]{2,1,0:T(8,128)(2,1)} %get-tuple-element.9), channel_id=1, source_target_pairs={{0,1},{1,2},{2,3},{3,4},{4,5},{5,6},{6,7},{8,9},{9,10},{10,11},{11... | collective-permute-start | bytes 1572872 | tf_op jit(solution)/shard_map/ppermute | solution.py:343
  70.7 0.0 copy-start.1
  70.7 2.1 %collective-permute-start.5 = (bf16[4,512,128]{2,1,0:T(8,128)(2,1)}, bf16[4,512,128]{2,1,0:T(8,128)(2,1)S(1)}, u32[]{:S(2)}, u32[]{:S(2)}) collective-permute-start(bf16[4,512,128]{2,1,0:T(8,128)(2,1)} %get-tuple-element.10), channel_id=1, source_target_pairs={{1,0},{2,1},{3,2},{4,3},{5,4},{6,5},{7,6},{9,8},{10,9},{11,10},{12... | collective-permute-start | bytes 1572872 | tf_op jit(solution)/shard_map/ppermute | solution.py:343
  72.8 4.3 %collective-permute-done.4 = bf16[4,512,128]{2,1,0:T(8,128)(2,1)S(1)} collective-permute-done((bf16[4,512,128]{2,1,0:T(8,128)(2,1)}, bf16[4,512,128]{2,1,0:T(8,128)(2,1)S(1)}, u32[]{:S(2)}, u32[]{:S(2)}) %collective-permute-start.4) | collective-permute-done | bytes 524320 | tf_op jit(solution)/shard_map/ppermute | solution.py:343
  77.2 4.7 %collective-permute-done.5 = bf16[4,512,128]{2,1,0:T(8,128)(2,1)S(1)} collective-permute-done((bf16[4,512,128]{2,1,0:T(8,128)(2,1)}, bf16[4,512,128]{2,1,0:T(8,128)(2,1)S(1)}, u32[]{:S(2)}, u32[]{:S(2)}) %collective-permute-start.5) | collective-permute-done | bytes 524320 | tf_op jit(solution)/shard_map/ppermute | solution.py:343
  81.9 1.3 %add_convert_fusion.1 = (bf16[4,128,256]{2,1,0:T(8,128)(2,1)S(1)}, bf16[4,128,256]{2,1,0:T(8,128)(2,1)S(1)}) fusion(f32[4,512,256]{2,1,0:T(8,128)} %get-tuple-element.8, bf16[4,128,128]{2,1,0:T(8,128)(2,1)S(1)} %get-tuple-element.15, bf16[4,128,128]{2,1,0:T(8,128)(2,1)S(1)} %get-tuple-element.13, bf16[4,128,128]{2,1,0:T(8,128)(2,1)S(1)} %get-tuple-element.16, ...), kind=kLoop, calls=%fused_computation.4 | loop fusion | flops 1572864 | bytes 2097152 | tf_op jit(solution)/shard_map/convert_element_type | solution.py:378
  83.2 1.9 %collective-permute-start.6 = (bf16[4,128,256]{2,1,0:T(8,128)(2,1)S(1)}, bf16[4,128,256]{2,1,0:T(8,128)(2,1)S(1)}, u32[]{:S(2)}, u32[]{:S(2)}) collective-permute-start(bf16[4,128,256]{2,1,0:T(8,128)(2,1)S(1)} %get-tuple-element.11), channel_id=1, source_target_pairs={{0,8},{8,16},{16,24},{24,32},{32,40},{40,48},{48,56},{56,64},{64,7... | collective-permute-start | bytes 786440 | tf_op jit(solution)/shard_map/ppermute | solution.py:343
  85.2 3.4 %collective-permute-start.7 = (bf16[4,128,256]{2,1,0:T(8,128)(2,1)S(1)}, bf16[4,128,256]{2,1,0:T(8,128)(2,1)S(1)}, u32[]{:S(2)}, u32[]{:S(2)}) collective-permute-start(bf16[4,128,256]{2,1,0:T(8,128)(2,1)S(1)} %get-tuple-element.12), channel_id=1, source_target_pairs={{8,0},{16,8},{24,16},{32,24},{40,32},{48,40},{56,48},{64,56},{72,6... | collective-permute-start | bytes 786440 | tf_op jit(solution)/shard_map/ppermute | solution.py:343
  88.6 1.8 %collective-permute-done.6 = bf16[4,128,256]{2,1,0:T(8,128)(2,1)S(1)} collective-permute-done((bf16[4,128,256]{2,1,0:T(8,128)(2,1)S(1)}, bf16[4,128,256]{2,1,0:T(8,128)(2,1)S(1)}, u32[]{:S(2)}, u32[]{:S(2)}) %collective-permute-start.6) | collective-permute-done | bytes 262176 | tf_op jit(solution)/shard_map/ppermute | solution.py:343
  90.3 4.0 %collective-permute-done.7 = bf16[4,128,256]{2,1,0:T(8,128)(2,1)S(1)} collective-permute-done((bf16[4,128,256]{2,1,0:T(8,128)(2,1)S(1)}, bf16[4,128,256]{2,1,0:T(8,128)(2,1)S(1)}, u32[]{:S(2)}, u32[]{:S(2)}) %collective-permute-start.7) | collective-permute-done | bytes 262176 | tf_op jit(solution)/shard_map/ppermute | solution.py:343
  94.4 0.0 copy-done.1
  94.4 1.1 %convert_add_fusion = f32[4,256,256]{2,1,0:T(8,128)} fusion(f32[4,512,256]{2,1,0:T(8,128)S(1)} %copy-done.1, bf16[4,256,128]{2,1,0:T(8,128)(2,1)S(1)} %slice.82, bf16[4,256,128]{2,1,0:T(8,128)(2,1)S(1)} %slice.81, bf16[4,128,256]{2,1,0:T(8,128)(2,1)S(1)} %collective-permute-done.7, bf16[4,128,256]{2,1,0:T(8,128)(2,1)S(1)} %collective-permute-done.6), kind=kLoop, calls=%fused_computation | loop fusion | flops 2621440 | bytes 3145728 | tf_op jit(solution)/shard_map/add | solution.py:380
  (9 shorter events, 0.3 us)
Async XLA Ops:
  1.3 16.1 %collective-permute-start.1 = (bf16[4,128,256]{2,1,0:T(8,128)(2,1)S(1)}, bf16[4,128,256]{2,1,0:T(8,128)(2,1)S(1)}, u32[]{:S(2)}, u32[]{:S(2)}) collective-permute-start(bf16[4,128,256]{2,1,0:T(8,128)(2,1)S(1)} %get-tuple-element.19), channel_id=1, source_target_pairs={{8,0},{16,8},{24,16},{32,24},{40,32},{48,40},{56,48},{64,56},{72,6... | collective-permute-start | bytes 786440 | tf_op jit(solution)/shard_map/ppermute | solution.py:343
  3.7 13.8 %collective-permute-start = (bf16[4,128,256]{2,1,0:T(8,128)(2,1)S(1)}, bf16[4,128,256]{2,1,0:T(8,128)(2,1)S(1)}, u32[]{:S(2)}, u32[]{:S(2)}) collective-permute-start(bf16[4,128,256]{2,1,0:T(8,128)(2,1)S(1)} %get-tuple-element.20), channel_id=1, source_target_pairs={{0,8},{8,16},{16,24},{24,32},{32,40},{40,48},{48,56},{56,64},{64,7... | collective-permute-start | bytes 786440 | tf_op jit(solution)/shard_map/ppermute | solution.py:343
  10.8 22.3 %all-to-all-start = ((bf16[8,272,256]{2,1,0:T(8,128)(2,1)}), bf16[8,272,256]{2,1,0:T(8,128)(2,1)S(1)}, u32[]{:S(2)}, u32[]{:S(2)}) async-start(bf16[8,272,256]{2,1,0:T(8,128)(2,1)} %shard_map.55), calls=%async_computation | async-start | bytes 2228224 | tf_op jit(solution)/shard_map/all_to_all | solution.py:358
  17.5 20.1 %copy-start.2 = (bf16[4,128,256]{2,1,0:T(8,128)(2,1)}, bf16[4,128,256]{2,1,0:T(8,128)(2,1)S(1)}, u32[]{:S(2)}) copy-start(bf16[4,128,256]{2,1,0:T(8,128)(2,1)S(1)} %collective-permute-done.1.down_hbm) | copy-start | bytes 786436
  17.6 20.0 %copy-start.3 = (bf16[4,128,256]{2,1,0:T(8,128)(2,1)}, bf16[4,128,256]{2,1,0:T(8,128)(2,1)S(1)}, u32[]{:S(2)}) copy-start(bf16[4,128,256]{2,1,0:T(8,128)(2,1)S(1)} %collective-permute-done.up_hbm) | copy-start | bytes 786436
  17.7 18.0 %collective-permute-start.2 = (bf16[4,512,128]{2,1,0:T(8,128)(2,1)S(1)}, bf16[4,512,128]{2,1,0:T(8,128)(2,1)S(1)}, u32[]{:S(2)}, u32[]{:S(2)}) collective-permute-start(bf16[4,512,128]{2,1,0:T(8,128)(2,1)S(1)} %pad_maximum_fusion), channel_id=1, source_target_pairs={{0,1},{1,2},{2,3},{3,4},{4,5},{5,6},{6,7},{8,9},{9,10},{10,11},{11... | collective-permute-start | bytes 1572872 | tf_op jit(solution)/shard_map/ppermute | solution.py:343
  21.3 16.3 %collective-permute-start.3 = (bf16[4,512,128]{2,1,0:T(8,128)(2,1)S(1)}, bf16[4,512,128]{2,1,0:T(8,128)(2,1)}, u32[]{:S(2)}, u32[]{:S(2)}) collective-permute-start(bf16[4,512,128]{2,1,0:T(8,128)(2,1)S(1)} %pad_maximum_fusion.1), channel_id=1, source_target_pairs={{1,0},{2,1},{3,2},{4,3},{5,4},{6,5},{7,6},{9,8},{10,9},{11,10},{12... | collective-permute-start | bytes 1572872 | tf_op jit(solution)/shard_map/ppermute | solution.py:343
  33.2 4.4 %copy-start = (bf16[8,272,256]{2,1,0:T(8,128)(2,1)}, bf16[8,272,256]{2,1,0:T(8,128)(2,1)S(1)}, u32[]{:S(2)}) copy-start(bf16[8,272,256]{2,1,0:T(8,128)(2,1)S(1)} %all-to-all-done.pat_hbm) | copy-start | bytes 3342340
  35.7 1.9 %copy-start.4 = (bf16[4,512,128]{2,1,0:T(8,128)(2,1)}, bf16[4,512,128]{2,1,0:T(8,128)(2,1)S(1)}, u32[]{:S(2)}) copy-start(bf16[4,512,128]{2,1,0:T(8,128)(2,1)S(1)} %collective-permute-done.2.west_hbm) | copy-start | bytes 1572868
  43.1 34.1 %collective-permute-start.4 = (bf16[4,512,128]{2,1,0:T(8,128)(2,1)}, bf16[4,512,128]{2,1,0:T(8,128)(2,1)S(1)}, u32[]{:S(2)}, u32[]{:S(2)}) collective-permute-start(bf16[4,512,128]{2,1,0:T(8,128)(2,1)} %get-tuple-element.9), channel_id=1, source_target_pairs={{0,1},{1,2},{2,3},{3,4},{4,5},{5,6},{6,7},{8,9},{9,10},{10,11},{11... | collective-permute-start | bytes 1572872 | tf_op jit(solution)/shard_map/ppermute | solution.py:343
  70.7 23.7 %copy-start.1 = (f32[4,512,256]{2,1,0:T(8,128)S(1)}, f32[4,512,256]{2,1,0:T(8,128)}, u32[]{:S(2)}) copy-start(f32[4,512,256]{2,1,0:T(8,128)} %get-tuple-element.8) | copy-start | bytes 6291460
  70.7 11.1 %collective-permute-start.5 = (bf16[4,512,128]{2,1,0:T(8,128)(2,1)}, bf16[4,512,128]{2,1,0:T(8,128)(2,1)S(1)}, u32[]{:S(2)}, u32[]{:S(2)}) collective-permute-start(bf16[4,512,128]{2,1,0:T(8,128)(2,1)} %get-tuple-element.10), channel_id=1, source_target_pairs={{1,0},{2,1},{3,2},{4,3},{5,4},{6,5},{7,6},{9,8},{10,9},{11,10},{12... | collective-permute-start | bytes 1572872 | tf_op jit(solution)/shard_map/ppermute | solution.py:343
  83.2 7.1 %collective-permute-start.6 = (bf16[4,128,256]{2,1,0:T(8,128)(2,1)S(1)}, bf16[4,128,256]{2,1,0:T(8,128)(2,1)S(1)}, u32[]{:S(2)}, u32[]{:S(2)}) collective-permute-start(bf16[4,128,256]{2,1,0:T(8,128)(2,1)S(1)} %get-tuple-element.11), channel_id=1, source_target_pairs={{0,8},{8,16},{16,24},{24,32},{32,40},{40,48},{48,56},{56,64},{64,7... | collective-permute-start | bytes 786440 | tf_op jit(solution)/shard_map/ppermute | solution.py:343
  85.2 9.2 %collective-permute-start.7 = (bf16[4,128,256]{2,1,0:T(8,128)(2,1)S(1)}, bf16[4,128,256]{2,1,0:T(8,128)(2,1)S(1)}, u32[]{:S(2)}, u32[]{:S(2)}) collective-permute-start(bf16[4,128,256]{2,1,0:T(8,128)(2,1)S(1)} %get-tuple-element.12), channel_id=1, source_target_pairs={{8,0},{16,8},{24,16},{32,24},{40,32},{48,40},{56,48},{64,56},{72,6... | collective-permute-start | bytes 786440 | tf_op jit(solution)/shard_map/ppermute | solution.py:343

commit v4 on v3

--- a/solution.py
+++ b/solution.py
@@ -67,13 +67,18 @@
 
 
 def windows_kernel(
-    half, where_ref, own_hbm, up_hbm, down_hbm, west_hbm, east_hbm, probe_hbm, pat_hbm, tab_hbm,
-    mid_hbm, wout_hbm, eout_hbm,
-    ext_ref, acc_ref, order_ref, own_ref, up_ref, down_ref, west_ref, east_ref, probe_ref, pat_ref,
-    tab_ref, mid_ref, wout_ref, eout_ref, in_sems, out_sems, *streams,
+    half, where_ref, own_hbm, up_hbm, down_hbm, west_hbm, east_hbm, probe_hbm, tab_hbm, *refs,
 ):
-    sources = (west_hbm, east_hbm, up_hbm, down_hbm, own_hbm, tab_hbm, probe_hbm, pat_hbm)
-    targets = (west_ref, east_ref, up_ref, down_ref, own_ref, tab_ref, probe_ref, pat_ref)
+    slots = where_ref.shape[0]
+    pat_hbms = refs[:slots]
+    mid_hbm, wout_hbm, eout_hbm = refs[slots : slots + 3]
+    (
+        ext_ref, acc_ref, order_ref, own_ref, up_ref, down_ref, west_ref, east_ref, probe_ref, pat_ref,
+        tab_ref, mid_ref, wout_ref, eout_ref, in_sems, out_sems, *streams,
+    ) = refs[slots + 3 :]
+    sources = (west_hbm, east_hbm, up_hbm, down_hbm, own_hbm, tab_hbm, probe_hbm) + pat_hbms
+    targets = (west_ref, east_ref, up_ref, down_ref, own_ref, tab_ref, probe_ref)
+    targets += tuple(pat_ref.at[k] for k in range(slots))
     loads = [
         pltpu.make_async_copy(source, into, in_sems.at[i])
         for i, (source, into) in enumerate(zip(sources, targets))
@@ -82,7 +87,6 @@
         load.start()
     slices, tile_y, tile_x = own_ref.shape
     width = probe_ref.shape[1]
-    slots = pat_ref.shape[0]
     rows = 64
     f32, bf16 = jnp.float32, jnp.bfloat16
     tall = tile_y + width
@@ -270,6 +274,7 @@
 def run_windows(where, own, up, down, west, east, probe, patterns, tables, interpret=False):
     slices, tile_y, tile_x = own.shape
     width = probe.shape[1]
+    slots = len(patterns)
     half = width // 2
     tall = tile_y + width
     f32, bf16 = jnp.float32, jnp.bfloat16
@@ -281,22 +286,22 @@
             jax.ShapeDtypeStruct((slices, tall, half), bf16),
             jax.ShapeDtypeStruct((slices, tall, half), bf16),
         ),
-        in_specs=[pl.BlockSpec(memory_space=pltpu.SMEM)] + [hbm] * 8,
+        in_specs=[pl.BlockSpec(memory_space=pltpu.SMEM)] + [hbm] * (7 + slots),
         out_specs=(hbm,) * 3,
         scratch_shapes=[
             pltpu.VMEM((slices, tall * PITCH, LANES), f32),
             pltpu.VMEM((slices, tall * PITCH, LANES), f32),
-            pltpu.SMEM((patterns.shape[0],), jnp.int32),
+            pltpu.SMEM((slots,), jnp.int32),
         ]
         + [
-            pltpu.VMEM(x.shape, x.dtype)
-            for x in (own, up, down, west, east, probe, patterns, tables)
+            pltpu.VMEM(x.shape, x.dtype) for x in (own, up, down, west, east, probe)
         ]
+        + [pltpu.VMEM((slots,) + patterns[0].shape, bf16), pltpu.VMEM(tables.shape, bf16)]
         + [
             pltpu.VMEM((slices, tall, tile_x), f32),
             pltpu.VMEM((slices, tall, half), bf16),
             pltpu.VMEM((slices, tall, half), bf16),
-            pltpu.SemaphoreType.DMA((8,)),
+            pltpu.SemaphoreType.DMA((7 + slots,)),
             pltpu.SemaphoreType.DMA((slices, 3)),
         ]
         + [
@@ -308,33 +313,42 @@
         * STREAMS,
         compiler_params=pltpu.CompilerParams(vmem_limit_bytes=56 << 20),
         interpret=interpret,
-    )(where, own, up, down, west, east, probe, patterns, tables)
-
-
-def parcel_kernel(centers_ref, pat_ref, sent_ref):
-    slots, _, width = sent_ref.shape
-    bf16 = jnp.bfloat16
+    )(where, own, up, down, west, east, probe, tables, *patterns)
+
+
+def parcel_kernel(me_ref, centers_ref, pat_ref, *sent_refs):
+    slots, width = len(sent_refs), pat_ref.shape[1]
+    count = pat_ref.shape[0]
     lane = lax.broadcasted_iota(jnp.int32, (SLOT_PAD, width), 1)
-    sent_ref[...] = jnp.zeros(sent_ref.shape, bf16)
-    for p in range(pat_ref.shape[0]):
-        owner = centers_ref[p, 1] // TILE
+    steps, infos = [], []
+    for p in range(count):
+        steps.append(lax.rem(centers_ref[p, 1] // TILE - me_ref[0] + slots, slots))
         row = centers_ref[p, 0] % TILE
         col = centers_ref[p, 1] % TILE
         info = jnp.where(lane == 0, row, jnp.where(lane == 1, col, jnp.where(lane == 2, 1, 0)))
-        sent_ref[owner, :width] = pat_ref[p]
-        sent_ref[owner, width:] = info.astype(jnp.float32).astype(bf16)
-
-
-def parcels(centers, patterns, slots):
+        infos.append(info.astype(jnp.float32).astype(jnp.bfloat16))
+    for k in range(slots):
+        sent_refs[k][...] = jnp.zeros(sent_refs[k].shape, jnp.bfloat16)
+        for p in range(count):
+
+            @pl.when(steps[p] == k)
+            def _(k=k, p=p):
+                sent_refs[k][:width] = pat_ref[p]
+                sent_refs[k][width:] = infos[p]
+
+
+def parcels(me, centers, patterns, slots):
     width = patterns.shape[1]
     vmem = pl.BlockSpec(memory_space=pltpu.VMEM)
+    smem = pl.BlockSpec(memory_space=pltpu.SMEM)
+    parcel = jax.ShapeDtypeStruct((width + SLOT_PAD, width), jnp.bfloat16)
     return pl.pallas_call(
         parcel_kernel,
-        out_shape=jax.ShapeDtypeStruct((slots, width + SLOT_PAD, width), jnp.bfloat16),
-        in_specs=[pl.BlockSpec(memory_space=pltpu.SMEM), vmem],
-        out_specs=vmem,
+        out_shape=(parcel,) * slots,
+        in_specs=[smem, smem, vmem],
+        out_specs=(vmem,) * slots,
         compiler_params=pltpu.CompilerParams(vmem_limit_bytes=56 << 20),
-    )(centers, patterns)
+    )(me, centers, patterns)
 
 
 def shift(cells, axis, step):
@@ -354,9 +368,12 @@
     up = shift(rounded[:, tile_y - half :], "ty", 1)
     down = shift(rounded[:, :half], "ty", -1)
 
-    sent = parcels(scan_centers, patterns, columns)
-    got = lax.all_to_all(sent, "tx", split_axis=0, concat_axis=0, tiled=True)
-    where = got[:, width, :3].astype(f32).astype(jnp.int32)
+    me = lax.axis_index("tx").astype(jnp.int32)[None]
+    got = [
+        parcel if k == 0 else lax.ppermute(parcel, "tx", [(i, (i + k) % columns) for i in range(columns)])
+        for k, parcel in enumerate(parcels(me, scan_centers, patterns, columns))
+    ]
+    where = jnp.stack([parcel[width, :3] for parcel in got]).astype(f32).astype(jnp.int32)
 
     def strip(cols):
         return jnp.concatenate([up[:, :, cols], rounded[:, :, cols], down[:, :, cols]], 1)

time: 97.1 us -> 109 us (1.12)
  the two profiles are of different devices: /device:TPU:29 before, /device:TPU:25 now
where the time goes in v4:
time: 109 us; the launch traced here: 107 us
  starting transfers between devices  50.8 us (47%)
  waiting for transfers between devices  28.7 us (26%)
  Pallas kernels  19.7 us (18%)
  other arithmetic  4.41 us (4%)
  local copies, waits for them, and re-layouts  3.25 us (3%)
    ppermute x8, starting transfers between devices, shift(): return lax.ppermute(cells, axis, pairs)  38.7 us
    pallas_call x1, Pallas kernels, run_windows(): pl.pallas_call(functools.partial(windows_kernel, half), out_shape=(jax.Sh...  17.7 us
    ppermute x8, waiting for transfers between devices, shift(): return lax.ppermute(cells, axis, pairs)  15.6 us
    ppermute x7, waiting for transfers between devices, per_device(): lax.ppermute(parcel, 'tx', [(i, (i + k) % columns) for i in range(columns)])  13.1 us
    ppermute x7, starting transfers between devices, per_device(): lax.ppermute(parcel, 'tx', [(i, (i + k) % columns) for i in range(columns)])  12.1 us
    unnamed x36, local copies, waits for them, and re-layouts  2.22 us
  transfers between devices with their start and end apart: 15, of which 8 were waited for; matrix products, arithmetic and copies ran while one was open for 2% of the time, Pallas kernels for 2%

profile of v4, /device:TPU:25, one launch (start us, length us, event | category | flops | bytes accessed | tf_op | source)
XLA Modules:
  0.0 107.3 jit_solution(4102547445056798418)
XLA Ops:
  0.0 1.3 %convert_element_type.29 = bf16[4,256,256]{2,1,0:T(8,128)(2,1)S(1)} convert(f32[4,256,256]{2,1,0:T(8,128)} %own_hbm.1) | non-fusion elementwise | flops 262144 | bytes 1572864 | tf_op jit(solution)/shard_map/convert_element_type | solution.py:367
  1.3 2.4 %collective-permute-start.8 = (bf16[4,128,256]{2,1,0:T(8,128)(2,1)S(1)}, bf16[4,128,256]{2,1,0:T(8,128)(2,1)S(1)}, u32[]{:S(2)}, u32[]{:S(2)}) collective-permute-start(bf16[4,128,256]{2,1,0:T(8,128)(2,1)S(1)} %get-tuple-element.35), channel_id=1, source_target_pairs={{8,0},{16,8},{24,16},{32,24},{40,32},{48,40},{56,48},{64,56},{72,6... | collective-permute-start | bytes 786440 | tf_op jit(solution)/shard_map/ppermute | solution.py:357
  3.7 5.0 %collective-permute-start.7 = (bf16[4,128,256]{2,1,0:T(8,128)(2,1)S(1)}, bf16[4,128,256]{2,1,0:T(8,128)(2,1)S(1)}, u32[]{:S(2)}, u32[]{:S(2)}) collective-permute-start(bf16[4,128,256]{2,1,0:T(8,128)(2,1)S(1)} %get-tuple-element.36), channel_id=1, source_target_pairs={{0,8},{8,16},{16,24},{24,32},{32,40},{40,48},{48,56},{56,64},{64,7... | collective-permute-start | bytes 786440 | tf_op jit(solution)/shard_map/ppermute | solution.py:357
  8.7 2.1 %shard_map.55 = (bf16[272,256]{1,0:T(8,128)(2,1)}, bf16[272,256]{1,0:T(8,128)(2,1)}, bf16[272,256]{1,0:T(8,128)(2,1)}, bf16[272,256]{1,0:T(8,128)(2,1)}, bf16[27...) custom-call(s32[1]{0:T(128)} %bitcast.me_ref, ...), custom_call_target="tpu_custom_call" | custom-call | tf_op jit(solution)/shard_map/pallas_call | solution.py:345
  10.8 0.0 copy-start.14
  10.8 0.0 copy-start.13
  10.8 2.8 %collective-permute-start = (bf16[272,256]{1,0:T(8,128)(2,1)}, bf16[272,256]{1,0:T(8,128)(2,1)S(1)}, u32[]{:S(2)}, u32[]{:S(2)}) collective-permute-start(bf16[272,256]{1,0:T(8,128)(2,1)} %get-tuple-element.17), channel_id=1, source_target_pairs={{0,1},{1,2},{2,3},{3,4},{4,5},{5,6},{6,7},{7,0},{8,9},{9,10},{10,1... | collective-permute-start | bytes 417800 | tf_op jit(solution)/shard_map/ppermute | solution.py:373
  13.6 0.1 fusion.2
  13.7 0.0 collective-permute-done.8.down_hbm
  13.8 0.0 collective-permute-done.7.up_hbm
  13.8 0.0 copy-start.2
  13.9 4.8 %collective-permute-start.9 = (bf16[4,512,128]{2,1,0:T(8,128)(2,1)S(1)}, bf16[4,512,128]{2,1,0:T(8,128)(2,1)S(1)}, u32[]{:S(2)}, u32[]{:S(2)}) collective-permute-start(bf16[4,512,128]{2,1,0:T(8,128)(2,1)S(1)} %pad_maximum_fusion), channel_id=1, source_target_pairs={{0,1},{1,2},{2,3},{3,4},{4,5},{5,6},{6,7},{8,9},{9,10},{10,11},{11... | collective-permute-start | bytes 1572872 | tf_op jit(solution)/shard_map/ppermute | solution.py:357
  18.8 1.9 %collective-permute-start.10 = (bf16[4,512,128]{2,1,0:T(8,128)(2,1)S(1)}, bf16[4,512,128]{2,1,0:T(8,128)(2,1)S(1)}, u32[]{:S(2)}, u32[]{:S(2)}) collective-permute-start(bf16[4,512,128]{2,1,0:T(8,128)(2,1)S(1)} %pad_maximum_fusion.1), channel_id=1, source_target_pairs={{1,0},{2,1},{3,2},{4,3},{5,4},{6,5},{7,6},{9,8},{10,9},{11,10},{12... | collective-permute-start | bytes 1572872 | tf_op jit(solution)/shard_map/ppermute | solution.py:357
  20.7 0.0 copy-done.17
  20.8 1.7 %collective-permute-start.1 = (bf16[272,256]{1,0:T(8,128)(2,1)S(1)}, bf16[272,256]{1,0:T(8,128)(2,1)S(1)}, u32[]{:S(2)}, u32[]{:S(2)}) collective-permute-start(bf16[272,256]{1,0:T(8,128)(2,1)S(1)} %copy-done.17), channel_id=1, source_target_pairs={{0,2},{1,3},{2,4},{3,5},{4,6},{5,7},{6,0},{7,1},{8,10},{9,11},{10,... | collective-permute-start | bytes 417800 | tf_op jit(solution)/shard_map/ppermute | solution.py:373
  22.5 3.7 %collective-permute-start.2 = (bf16[272,256]{1,0:T(8,128)(2,1)S(1)}, bf16[272,256]{1,0:T(8,128)(2,1)S(1)}, u32[]{:S(2)}, u32[]{:S(2)}) collective-permute-start(bf16[272,256]{1,0:T(8,128)(2,1)S(1)} %copy-done.16), channel_id=1, source_target_pairs={{0,3},{1,4},{2,5},{3,6},{4,7},{5,0},{6,1},{7,2},{8,11},{9,12},{10,... | collective-permute-start | bytes 417800 | tf_op jit(solution)/shard_map/ppermute | solution.py:373
  26.1 0.0 collective-permute-done.refs_1_
  26.1 0.1 collective-permute-start.3
  26.2 2.8 %collective-permute-done.1.refs_2_ = bf16[272,256]{1,0:T(8,128)(2,1)S(1)} collective-permute-done((bf16[272,256]{1,0:T(8,128)(2,1)S(1)}, bf16[272,256]{1,0:T(8,128)(2,1)S(1)}, u32[]{:S(2)}, u32[]{:S(2)}) %collective-permute-start.1) | collective-permute-done | bytes 139296 | tf_op jit(solution)/shard_map/ppermute | solution.py:373
  29.0 0.0 copy-done.14
  29.0 2.3 %collective-permute-start.4 = (bf16[272,256]{1,0:T(8,128)(2,1)S(1)}, bf16[272,256]{1,0:T(8,128)(2,1)S(1)}, u32[]{:S(2)}, u32[]{:S(2)}) collective-permute-start(bf16[272,256]{1,0:T(8,128)(2,1)S(1)} %copy-done.14), channel_id=1, source_target_pairs={{0,5},{1,6},{2,7},{3,0},{4,1},{5,2},{6,3},{7,4},{8,13},{9,14},{10,... | collective-permute-start | bytes 417800 | tf_op jit(solution)/shard_map/ppermute | solution.py:373
  31.3 0.8 collective-permute-done.2.refs_3_
  32.1 1.6 %collective-permute-start.5 = (bf16[272,256]{1,0:T(8,128)(2,1)S(1)}, bf16[272,256]{1,0:T(8,128)(2,1)S(1)}, u32[]{:S(2)}, u32[]{:S(2)}) collective-permute-start(bf16[272,256]{1,0:T(8,128)(2,1)S(1)} %copy-done.13), channel_id=1, source_target_pairs={{0,6},{1,7},{2,0},{3,1},{4,2},{5,3},{6,4},{7,5},{8,14},{9,15},{10,... | collective-permute-start | bytes 417800 | tf_op jit(solution)/shard_map/ppermute | solution.py:373
  33.7 5.0 %collective-permute-done.3.refs_4_ = bf16[272,256]{1,0:T(8,128)(2,1)S(1)} collective-permute-done((bf16[272,256]{1,0:T(8,128)(2,1)S(1)}, bf16[272,256]{1,0:T(8,128)(2,1)S(1)}, u32[]{:S(2)}, u32[]{:S(2)}) %collective-permute-start.3) | collective-permute-done | bytes 139296 | tf_op jit(solution)/shard_map/ppermute | solution.py:373
  38.7 0.0 collective-permute-start.6
  38.7 0.7 slice.75
  39.4 0.0 collective-permute-done.4.refs_5_
  39.5 0.0 collective-permute-done.5.refs_6_
  39.5 0.0 copy-start.10
  39.5 4.5 %collective-permute-done.6.refs_7_ = bf16[272,256]{1,0:T(8,128)(2,1)S(1)} collective-permute-done((bf16[272,256]{1,0:T(8,128)(2,1)S(1)}, bf16[272,256]{1,0:T(8,128)(2,1)S(1)}, u32[]{:S(2)}, u32[]{:S(2)}) %collective-permute-start.6) | collective-permute-done | bytes 139296 | tf_op jit(solution)/shard_map/ppermute | solution.py:373
  44.0 0.7 copy-done.11
  44.7 0.6 convert_convert_fusion.where_ref
  45.3 0.0 collective-permute-done.9.west_hbm
  45.3 0.0 collective-permute-done.10.east_hbm
  45.4 0.7 copy-done.3
  46.1 0.8 copy-done.4
  46.9 17.7 %shard_map.56 = (f32[4,512,256]{2,1,0:T(8,128)}, bf16[4,512,128]{2,1,0:T(8,128)(2,1)}, bf16[4,512,128]{2,1,0:T(8,128)(2,1)}) custom-call(s32[8,3]{1,0:T(8,128)} %convert_convert_fusion.where_ref, f32[4,256,256]{2,1,0:T(8,128)} %own_hbm.1, bf16[4,128,256]{2,1,0:T(8,128)(2,1)} %copy-done.2, bf16[4,128,256]{2,1,0:T(8,128)(2,1)} %copy-done.1, ...), custom_call_target="tpu_custom_call" | custom-call | tf_op jit(solution)/shard_map/pallas_call | solution.py:282
  64.6 1.9 %collective-permute-start.11 = (bf16[4,512,128]{2,1,0:T(8,128)(2,1)}, bf16[4,512,128]{2,1,0:T(8,128)(2,1)S(1)}, u32[]{:S(2)}, u32[]{:S(2)}) collective-permute-start(bf16[4,512,128]{2,1,0:T(8,128)(2,1)} %get-tuple-element.25), channel_id=1, source_target_pairs={{0,1},{1,2},{2,3},{3,4},{4,5},{5,6},{6,7},{8,9},{9,10},{10,11},{11... | collective-permute-start | bytes 1572872 | tf_op jit(solution)/shard_map/ppermute | solution.py:357
  66.5 2.6 %collective-permute-start.12 = (bf16[4,512,128]{2,1,0:T(8,128)(2,1)}, bf16[4,512,128]{2,1,0:T(8,128)(2,1)S(1)}, u32[]{:S(2)}, u32[]{:S(2)}) collective-permute-start(bf16[4,512,128]{2,1,0:T(8,128)(2,1)} %get-tuple-element.26), channel_id=1, source_target_pairs={{1,0},{2,1},{3,2},{4,3},{5,4},{6,5},{7,6},{9,8},{10,9},{11,10},{12... | collective-permute-start | bytes 1572872 | tf_op jit(solution)/shard_map/ppermute | solution.py:357
  69.1 3.8 %collective-permute-done.11 = bf16[4,512,128]{2,1,0:T(8,128)(2,1)S(1)} collective-permute-done((bf16[4,512,128]{2,1,0:T(8,128)(2,1)}, bf16[4,512,128]{2,1,0:T(8,128)(2,1)S(1)}, u32[]{:S(2)}, u32[]{:S(2)}) %collective-permute-start.11) | collective-permute-done | bytes 524320 | tf_op jit(solution)/shard_map/ppermute | solution.py:357
  72.9 4.5 %collective-permute-done.12 = bf16[4,512,128]{2,1,0:T(8,128)(2,1)S(1)} collective-permute-done((bf16[4,512,128]{2,1,0:T(8,128)(2,1)}, bf16[4,512,128]{2,1,0:T(8,128)(2,1)S(1)}, u32[]{:S(2)}, u32[]{:S(2)}) %collective-permute-start.12) | collective-permute-done | bytes 524320 | tf_op jit(solution)/shard_map/ppermute | solution.py:357
  77.5 1.3 %add_convert_fusion.1 = (bf16[4,128,256]{2,1,0:T(8,128)(2,1)S(1)}, bf16[4,128,256]{2,1,0:T(8,128)(2,1)S(1)}) fusion(f32[4,512,256]{2,1,0:T(8,128)} %get-tuple-element.24, bf16[4,128,128]{2,1,0:T(8,128)(2,1)S(1)} %get-tuple-element.31, bf16[4,128,128]{2,1,0:T(8,128)(2,1)S(1)} %get-tuple-element.29, bf16[4,128,128]{2,1,0:T(8,128)(2,1)S(1)} %get-tuple-element.32, ...), kind=kLoop, calls=%fused_computation.4 | loop fusion | flops 1572864 | bytes 2097152 | tf_op jit(solution)/shard_map/convert_element_type | solution.py:395
  78.8 18.1 %collective-permute-start.13 = (bf16[4,128,256]{2,1,0:T(8,128)(2,1)S(1)}, bf16[4,128,256]{2,1,0:T(8,128)(2,1)S(1)}, u32[]{:S(2)}, u32[]{:S(2)}) collective-permute-start(bf16[4,128,256]{2,1,0:T(8,128)(2,1)S(1)} %get-tuple-element.27), channel_id=1, source_target_pairs={{0,8},{8,16},{16,24},{24,32},{32,40},{40,48},{48,56},{56,64},{64,7... | collective-permute-start | bytes 786440 | tf_op jit(solution)/shard_map/ppermute | solution.py:357
  97.0 1.9 %collective-permute-start.14 = (bf16[4,128,256]{2,1,0:T(8,128)(2,1)S(1)}, bf16[4,128,256]{2,1,0:T(8,128)(2,1)S(1)}, u32[]{:S(2)}, u32[]{:S(2)}) collective-permute-start(bf16[4,128,256]{2,1,0:T(8,128)(2,1)S(1)} %get-tuple-element.28), channel_id=1, source_target_pairs={{8,0},{16,8},{24,16},{32,24},{40,32},{48,40},{56,48},{64,56},{72,6... | collective-permute-start | bytes 786440 | tf_op jit(solution)/shard_map/ppermute | solution.py:357
  98.9 1.3 %collective-permute-done.13 = bf16[4,128,256]{2,1,0:T(8,128)(2,1)S(1)} collective-permute-done((bf16[4,128,256]{2,1,0:T(8,128)(2,1)S(1)}, bf16[4,128,256]{2,1,0:T(8,128)(2,1)S(1)}, u32[]{:S(2)}, u32[]{:S(2)}) %collective-permute-start.13) | collective-permute-done | bytes 262176 | tf_op jit(solution)/shard_map/ppermute | solution.py:357
  100.2 5.9 %collective-permute-done.14 = bf16[4,128,256]{2,1,0:T(8,128)(2,1)S(1)} collective-permute-done((bf16[4,128,256]{2,1,0:T(8,128)(2,1)S(1)}, bf16[4,128,256]{2,1,0:T(8,128)(2,1)S(1)}, u32[]{:S(2)}, u32[]{:S(2)}) %collective-permute-start.14) | collective-permute-done | bytes 262176 | tf_op jit(solution)/shard_map/ppermute | solution.py:357
  106.2 0.0 copy-done
  106.2 1.1 %convert_add_fusion = f32[4,256,256]{2,1,0:T(8,128)} fusion(f32[4,512,256]{2,1,0:T(8,128)S(1)} %copy-done, bf16[4,256,128]{2,1,0:T(8,128)(2,1)S(1)} %slice.116, bf16[4,256,128]{2,1,0:T(8,128)(2,1)S(1)} %slice.115, bf16[4,128,256]{2,1,0:T(8,128)(2,1)S(1)} %collective-permute-done.14, bf16[4,128,256]{2,1,0:T(8,128)(2,1)S(1)} %collective-permute-done.13), kind=kLoop, calls=%fused_computation | loop fusion | flops 2621440 | bytes 3145728 | tf_op jit(solution)/shard_map/add | solution.py:397
  (43 shorter events, 0.4 us)
Async XLA Ops:
  1.3 12.4 %collective-permute-start.8 = (bf16[4,128,256]{2,1,0:T(8,128)(2,1)S(1)}, bf16[4,128,256]{2,1,0:T(8,128)(2,1)S(1)}, u32[]{:S(2)}, u32[]{:S(2)}) collective-permute-start(bf16[4,128,256]{2,1,0:T(8,128)(2,1)S(1)} %get-tuple-element.35), channel_id=1, source_target_pairs={{8,0},{16,8},{24,16},{32,24},{40,32},{48,40},{56,48},{64,56},{72,6... | collective-permute-start | bytes 786440 | tf_op jit(solution)/shard_map/ppermute | solution.py:357
  3.7 10.1 %collective-permute-start.7 = (bf16[4,128,256]{2,1,0:T(8,128)(2,1)S(1)}, bf16[4,128,256]{2,1,0:T(8,128)(2,1)S(1)}, u32[]{:S(2)}, u32[]{:S(2)}) collective-permute-start(bf16[4,128,256]{2,1,0:T(8,128)(2,1)S(1)} %get-tuple-element.36), channel_id=1, source_target_pairs={{0,8},{8,16},{16,24},{24,32},{32,40},{40,48},{48,56},{56,64},{64,7... | collective-permute-start | bytes 786440 | tf_op jit(solution)/shard_map/ppermute | solution.py:357
  10.8 9.9 %copy-start.17 = (bf16[272,256]{1,0:T(8,128)(2,1)S(1)}, bf16[272,256]{1,0:T(8,128)(2,1)}, u32[]{:S(2)}) copy-start(bf16[272,256]{1,0:T(8,128)(2,1)} %get-tuple-element.18) | copy-start | bytes 417796
  10.8 11.6 %copy-start.16 = (bf16[272,256]{1,0:T(8,128)(2,1)S(1)}, bf16[272,256]{1,0:T(8,128)(2,1)}, u32[]{:S(2)}) copy-start(bf16[272,256]{1,0:T(8,128)(2,1)} %get-tuple-element.19) | copy-start | bytes 417796
  10.8 15.3 %copy-start.15 = (bf16[272,256]{1,0:T(8,128)(2,1)S(1)}, bf16[272,256]{1,0:T(8,128)(2,1)}, u32[]{:S(2)}) copy-start(bf16[272,256]{1,0:T(8,128)(2,1)} %get-tuple-element.20) | copy-start | bytes 417796
  10.8 18.2 %copy-start.14 = (bf16[272,256]{1,0:T(8,128)(2,1)S(1)}, bf16[272,256]{1,0:T(8,128)(2,1)}, u32[]{:S(2)}) copy-start(bf16[272,256]{1,0:T(8,128)(2,1)} %get-tuple-element.21) | copy-start | bytes 417796
  10.8 21.2 %copy-start.13 = (bf16[272,256]{1,0:T(8,128)(2,1)S(1)}, bf16[272,256]{1,0:T(8,128)(2,1)}, u32[]{:S(2)}) copy-start(bf16[272,256]{1,0:T(8,128)(2,1)} %get-tuple-element.22) | copy-start | bytes 417796
  10.8 27.9 %copy-start.12 = (bf16[272,256]{1,0:T(8,128)(2,1)S(1)}, bf16[272,256]{1,0:T(8,128)(2,1)}, u32[]{:S(2)}) copy-start(bf16[272,256]{1,0:T(8,128)(2,1)} %get-tuple-element.23) | copy-start | bytes 417796
  10.8 15.3 %collective-permute-start = (bf16[272,256]{1,0:T(8,128)(2,1)}, bf16[272,256]{1,0:T(8,128)(2,1)S(1)}, u32[]{:S(2)}, u32[]{:S(2)}) collective-permute-start(bf16[272,256]{1,0:T(8,128)(2,1)} %get-tuple-element.17), channel_id=1, source_target_pairs={{0,1},{1,2},{2,3},{3,4},{4,5},{5,6},{6,7},{7,0},{8,9},{9,10},{10,1... | collective-permute-start | bytes 417800 | tf_op jit(solution)/shard_map/ppermute | solution.py:373
  13.7 31.6 %copy-start.1 = (bf16[4,128,256]{2,1,0:T(8,128)(2,1)}, bf16[4,128,256]{2,1,0:T(8,128)(2,1)S(1)}, u32[]{:S(2)}) copy-start(bf16[4,128,256]{2,1,0:T(8,128)(2,1)S(1)} %collective-permute-done.8.down_hbm) | copy-start | bytes 786436
  13.8 31.5 %copy-start.2 = (bf16[4,128,256]{2,1,0:T(8,128)(2,1)}, bf16[4,128,256]{2,1,0:T(8,128)(2,1)S(1)}, u32[]{:S(2)}) copy-start(bf16[4,128,256]{2,1,0:T(8,128)(2,1)S(1)} %collective-permute-done.7.up_hbm) | copy-start | bytes 786436
  13.9 31.4 %collective-permute-start.9 = (bf16[4,512,128]{2,1,0:T(8,128)(2,1)S(1)}, bf16[4,512,128]{2,1,0:T(8,128)(2,1)S(1)}, u32[]{:S(2)}, u32[]{:S(2)}) collective-permute-start(bf16[4,512,128]{2,1,0:T(8,128)(2,1)S(1)} %pad_maximum_fusion), channel_id=1, source_target_pairs={{0,1},{1,2},{2,3},{3,4},{4,5},{5,6},{6,7},{8,9},{9,10},{10,11},{11... | collective-permute-start | bytes 1572872 | tf_op jit(solution)/shard_map/ppermute | solution.py:357
  18.8 26.5 %collective-permute-start.10 = (bf16[4,512,128]{2,1,0:T(8,128)(2,1)S(1)}, bf16[4,512,128]{2,1,0:T(8,128)(2,1)S(1)}, u32[]{:S(2)}, u32[]{:S(2)}) collective-permute-start(bf16[4,512,128]{2,1,0:T(8,128)(2,1)S(1)} %pad_maximum_fusion.1), channel_id=1, source_target_pairs={{1,0},{2,1},{3,2},{4,3},{5,4},{6,5},{7,6},{9,8},{10,9},{11,10},{12... | collective-permute-start | bytes 1572872 | tf_op jit(solution)/shard_map/ppermute | solution.py:357
  20.8 8.3 %collective-permute-start.1 = (bf16[272,256]{1,0:T(8,128)(2,1)S(1)}, bf16[272,256]{1,0:T(8,128)(2,1)S(1)}, u32[]{:S(2)}, u32[]{:S(2)}) collective-permute-start(bf16[272,256]{1,0:T(8,128)(2,1)S(1)} %copy-done.17), channel_id=1, source_target_pairs={{0,2},{1,3},{2,4},{3,5},{4,6},{5,7},{6,0},{7,1},{8,10},{9,11},{10,... | collective-permute-start | bytes 417800 | tf_op jit(solution)/shard_map/ppermute | solution.py:373
  22.5 9.6 %collective-permute-start.2 = (bf16[272,256]{1,0:T(8,128)(2,1)S(1)}, bf16[272,256]{1,0:T(8,128)(2,1)S(1)}, u32[]{:S(2)}, u32[]{:S(2)}) collective-permute-start(bf16[272,256]{1,0:T(8,128)(2,1)S(1)} %copy-done.16), channel_id=1, source_target_pairs={{0,3},{1,4},{2,5},{3,6},{4,7},{5,0},{6,1},{7,2},{8,11},{9,12},{10,... | collective-permute-start | bytes 417800 | tf_op jit(solution)/shard_map/ppermute | solution.py:373
  26.1 19.2 %copy-start.5 = (bf16[272,256]{1,0:T(8,128)(2,1)}, bf16[272,256]{1,0:T(8,128)(2,1)S(1)}, u32[]{:S(2)}) copy-start(bf16[272,256]{1,0:T(8,128)(2,1)S(1)} %collective-permute-done.refs_1_) | copy-start | bytes 417796
  26.1 12.6 %collective-permute-start.3 = (bf16[272,256]{1,0:T(8,128)(2,1)S(1)}, bf16[272,256]{1,0:T(8,128)(2,1)S(1)}, u32[]{:S(2)}, u32[]{:S(2)}) collective-permute-start(bf16[272,256]{1,0:T(8,128)(2,1)S(1)} %copy-done.15), channel_id=1, source_target_pairs={{0,4},{1,5},{2,6},{3,7},{4,0},{5,1},{6,2},{7,3},{8,12},{9,13},{10,... | collective-permute-start | bytes 417800 | tf_op jit(solution)/shard_map/ppermute | solution.py:373
  29.0 16.3 %copy-start.6 = (bf16[272,256]{1,0:T(8,128)(2,1)}, bf16[272,256]{1,0:T(8,128)(2,1)S(1)}, u32[]{:S(2)}) copy-start(bf16[272,256]{1,0:T(8,128)(2,1)S(1)} %collective-permute-done.1.refs_2_) | copy-start | bytes 417796
  29.0 10.4 %collective-permute-start.4 = (bf16[272,256]{1,0:T(8,128)(2,1)S(1)}, bf16[272,256]{1,0:T(8,128)(2,1)S(1)}, u32[]{:S(2)}, u32[]{:S(2)}) collective-permute-start(bf16[272,256]{1,0:T(8,128)(2,1)S(1)} %copy-done.14), channel_id=1, source_target_pairs={{0,5},{1,6},{2,7},{3,0},{4,1},{5,2},{6,3},{7,4},{8,13},{9,14},{10,... | collective-permute-start | bytes 417800 | tf_op jit(solution)/shard_map/ppermute | solution.py:373
  32.1 13.3 %copy-start.7 = (bf16[272,256]{1,0:T(8,128)(2,1)}, bf16[272,256]{1,0:T(8,128)(2,1)S(1)}, u32[]{:S(2)}) copy-start(bf16[272,256]{1,0:T(8,128)(2,1)S(1)} %collective-permute-done.2.refs_3_) | copy-start | bytes 417796
  32.1 7.4 %collective-permute-start.5 = (bf16[272,256]{1,0:T(8,128)(2,1)S(1)}, bf16[272,256]{1,0:T(8,128)(2,1)S(1)}, u32[]{:S(2)}, u32[]{:S(2)}) collective-permute-start(bf16[272,256]{1,0:T(8,128)(2,1)S(1)} %copy-done.13), channel_id=1, source_target_pairs={{0,6},{1,7},{2,0},{3,1},{4,2},{5,3},{6,4},{7,5},{8,14},{9,15},{10,... | collective-permute-start | bytes 417800 | tf_op jit(solution)/shard_map/ppermute | solution.py:373
  38.7 6.6 %copy-start.8 = (bf16[272,256]{1,0:T(8,128)(2,1)}, bf16[272,256]{1,0:T(8,128)(2,1)S(1)}, u32[]{:S(2)}) copy-start(bf16[272,256]{1,0:T(8,128)(2,1)S(1)} %collective-permute-done.3.refs_4_) | copy-start | bytes 417796
  38.7 5.3 %collective-permute-start.6 = (bf16[272,256]{1,0:T(8,128)(2,1)S(1)}, bf16[272,256]{1,0:T(8,128)(2,1)S(1)}, u32[]{:S(2)}, u32[]{:S(2)}) collective-permute-start(bf16[272,256]{1,0:T(8,128)(2,1)S(1)} %copy-done.12), channel_id=1, source_target_pairs={{0,7},{1,0},{2,1},{3,2},{4,3},{5,4},{6,5},{7,6},{8,15},{9,8},{10,9... | collective-permute-start | bytes 417800 | tf_op jit(solution)/shard_map/ppermute | solution.py:373
  39.5 5.9 %copy-start.9 = (bf16[272,256]{1,0:T(8,128)(2,1)}, bf16[272,256]{1,0:T(8,128)(2,1)S(1)}, u32[]{:S(2)}) copy-start(bf16[272,256]{1,0:T(8,128)(2,1)S(1)} %collective-permute-done.4.refs_5_) | copy-start | bytes 417796
  39.5 5.9 %copy-start.10 = (bf16[272,256]{1,0:T(8,128)(2,1)}, bf16[272,256]{1,0:T(8,128)(2,1)S(1)}, u32[]{:S(2)}) copy-start(bf16[272,256]{1,0:T(8,128)(2,1)S(1)} %collective-permute-done.5.refs_6_) | copy-start | bytes 417796
  44.0 0.7 copy-start.11
  45.3 0.8 copy-start.3
  46.1 0.8 copy-start.4
  64.6 8.3 %collective-permute-start.11 = (bf16[4,512,128]{2,1,0:T(8,128)(2,1)}, bf16[4,512,128]{2,1,0:T(8,128)(2,1)S(1)}, u32[]{:S(2)}, u32[]{:S(2)}) collective-permute-start(bf16[4,512,128]{2,1,0:T(8,128)(2,1)} %get-tuple-element.25), channel_id=1, source_target_pairs={{0,1},{1,2},{2,3},{3,4},{4,5},{5,6},{6,7},{8,9},{9,10},{10,11},{11... | collective-permute-start | bytes 1572872 | tf_op jit(solution)/shard_map/ppermute | solution.py:357
  66.5 39.7 %copy-start = (f32[4,512,256]{2,1,0:T(8,128)S(1)}, f32[4,512,256]{2,1,0:T(8,128)}, u32[]{:S(2)}) copy-start(f32[4,512,256]{2,1,0:T(8,128)} %get-tuple-element.24) | copy-start | bytes 6291460
  66.5 11.0 %collective-permute-start.12 = (bf16[4,512,128]{2,1,0:T(8,128)(2,1)}, bf16[4,512,128]{2,1,0:T(8,128)(2,1)S(1)}, u32[]{:S(2)}, u32[]{:S(2)}) collective-permute-start(bf16[4,512,128]{2,1,0:T(8,128)(2,1)} %get-tuple-element.26), channel_id=1, source_target_pairs={{1,0},{2,1},{3,2},{4,3},{5,4},{6,5},{7,6},{9,8},{10,9},{11,10},{12... | collective-permute-start | bytes 1572872 | tf_op jit(solution)/shard_map/ppermute | solution.py:357
  78.8 21.4 %collective-permute-start.13 = (bf16[4,128,256]{2,1,0:T(8,128)(2,1)S(1)}, bf16[4,128,256]{2,1,0:T(8,128)(2,1)S(1)}, u32[]{:S(2)}, u32[]{:S(2)}) collective-permute-start(bf16[4,128,256]{2,1,0:T(8,128)(2,1)S(1)} %get-tuple-element.27), channel_id=1, source_target_pairs={{0,8},{8,16},{16,24},{24,32},{32,40},{40,48},{48,56},{56,64},{64,7... | collective-permute-start | bytes 786440 | tf_op jit(solution)/shard_map/ppermute | solution.py:357
  97.0 9.2 %collective-permute-start.14 = (bf16[4,128,256]{2,1,0:T(8,128)(2,1)S(1)}, bf16[4,128,256]{2,1,0:T(8,128)(2,1)S(1)}, u32[]{:S(2)}, u32[]{:S(2)}) collective-permute-start(bf16[4,128,256]{2,1,0:T(8,128)(2,1)S(1)} %get-tuple-element.28), channel_id=1, source_target_pairs={{8,0},{16,8},{24,16},{32,24},{40,32},{48,40},{56,48},{64,56},{72,6... | collective-permute-start | bytes 786440 | tf_op jit(solution)/shard_map/ppermute | solution.py:357
